TPU v7x, 32 devices: a whole 2x2x4 slice. The times are simulated.
32 devices in a mesh: groups: 2 (over y), gx: 8 (over z, x), gy: 2 (over core).
Axes of the slice: x: 2, y: 2, z: 4, core: 2. Of those that a mesh axis runs over, the one named last changes fastest.
Arguments:
- voxels: bfloat16 [16, 128, 128, 64], P(('groups', 'gx'), 'gy'), parts along dimension 0, may hold values from -6 to 6
- occupancy: int32 [16, 128, 128], P(('groups', 'gx'), 'gy'), parts along dimension 0, may hold values 0 or 1
- row_weights: bfloat16 [8, 64], P('gx'), may hold values from -2 to 2
- column_weights: bfloat16 [128, 64], P('gy'), may hold values from -0.5 to 0.5
- depth_weights: bfloat16 [128, 64], replicated, may hold values from -0.5 to 0.5
- plane_kernels: bfloat16 [3, 2, 3, 3, 64, 64], replicated, may hold values from -0.25 to 0.25
- expand_weight: bfloat16 [64, 128], replicated, may hold values from -0.75 to 0.75
- shrink_weight: bfloat16 [128, 64], replicated, may hold values from -1 to 1
Outputs:
- updated: bfloat16 [16, 128, 128, 64], P(('groups', 'gx'), 'gy'), parts along dimension 0
There are 2 independent parts, one for each index of `groups`. A program takes and returns all parts, laid end to end along the dimension named above; an argument that names none is the same for every part. Nothing has to cross between parts.
All inputs are finite; a program needn't handle non-finite values. No bound on the sum of `occupancy` on one device may be relied on, other than what follows from the above.
Results may differ from a plain program's by a relative error of at most 0.015.
Values may be sent and summed in bfloat16 or wider, within the bound.
A program may use at most 64 MiB of HBM per device.

v0:
```python
import functools

import jax
import jax.numpy as jnp
from jax import lax
from jax.experimental import pallas as pl
from jax.experimental.pallas import tpu as pltpu
from jax.sharding import PartitionSpec as P

MESH = pl.DeviceIdType.MESH
reach = 2
cuts = 2

product_scale = 8.0


def with_halo(cells, sides, width):
    for axis, dim in sides:
        count = lax.axis_size(axis)
        ends = count - 1
        head = lax.slice_in_dim(cells, 0, width, axis=dim)
        tail = lax.slice_in_dim(cells, cells.shape[dim] - width, cells.shape[dim], axis=dim)
        cells = jnp.concatenate(
            [
                lax.ppermute(tail, axis, [(i, (i + 1) % count) for i in range(ends)]),
                cells,
                lax.ppermute(head, axis, [((i + 1) % count, i) for i in range(ends)]),
            ],
            axis=dim,
        )
    return cells


def conv_valid(padded, kernel):
    rows = padded.shape[0] - 2
    cols = padded.shape[1] - 2
    total = jnp.zeros((rows, cols, kernel.shape[-1]), jnp.float32)
    for row_off in range(3):
        for col_off in range(3):
            window = padded[row_off : row_off + rows, col_off : col_off + cols]
            total = total + jnp.einsum(
                "ijc,co->ijo", window, kernel[row_off, col_off], preferred_element_type=jnp.float32
            )
    return total


def plane_block(plane, kernels, extend):
    inner = jax.nn.silu(conv_valid(extend(plane), kernels[0])).astype(jnp.bfloat16)
    return conv_valid(extend(inner), kernels[1]).astype(jnp.bfloat16)


def rim_xy(plane):
    return with_halo(plane, (("gx", 0), ("gy", 1)), 1)


def rim_xz(plane):
    padded = with_halo(plane, (("gx", 0),), 1)
    return jnp.pad(padded, ((0, 0), (1, 1), (0, 0)))


def rim_yz(plane):
    padded = with_halo(plane, (("gy", 0),), 1)
    return jnp.pad(padded, ((0, 0), (1, 1), (0, 0)))


def conv_row(window, weight):
    taps = jnp.dot(weight, window, preferred_element_type=jnp.float32)
    chans = taps.shape[0] // 3
    cols = taps.shape[1]
    lane = lax.broadcasted_iota(jnp.int32, (chans, cols), 1)
    left = pltpu.roll(taps[:chans], 1, 1)
    right = pltpu.roll(taps[2 * chans :], cols - 1, 1)
    left = jnp.where(lane == 0, 0.0, left)
    right = jnp.where(lane == cols - 1, 0.0, right)
    return taps[chans : 2 * chans] + left + right


def silu(v):
    return v / (1.0 + jnp.exp(-v))


def identity(size):
    row = lax.broadcasted_iota(jnp.int32, (size, size), 0)
    col = lax.broadcasted_iota(jnp.int32, (size, size), 1)
    return jnp.where(row == col, 1.0, 0.0)


def flipped(x):
    eye = identity(x.shape[1]).astype(x.dtype)
    return lax.dot_general(eye, x, (((1,), (1,)), ((), ())), preferred_element_type=jnp.float32)


def column(x, at):
    lane = lax.broadcasted_iota(jnp.int32, x.shape, 1)
    return jnp.sum(jnp.where(lane == at, x, 0.0), axis=1, keepdims=True)


def block_kernel(
    n, voxels, occupancy, row_weights, column_weights, depth_weights, kernels_in, expand, shrink, updated,
    plane_kernels, fetch_s,
    part, rows_in, weights, wide, yz_out, xy_out, xz_out, row_sums, turned,
    pair_in, pair_sum, line_in, yz_sum, yz_plane, yz_inner, row_slots, row_plane, row_inner,
    pair_s, pair_r, line_s, line_r, halo_s, halo_r, row_s, row_r, spread_s, spread_r, cross_s, cross_r,
):
    me = lax.axis_index("gx")
    g = lax.axis_index("gy")
    m = n // 2
    a = me // 2
    b = me % 2
    count, chans, cols = part.shape
    rows = count // n
    bf = jnp.bfloat16

    def feature_row(y):
        return voxels[y].astype(jnp.float32) * occupancy[pl.ds(y, 1), :].astype(jnp.float32)

    def piece(bb, aa):
        return bb * m + aa + bb * (m - 1 - 2 * aa)

    def owner(j):
        bb = j // m
        aa = j % m
        return (aa + bb * (m - 1 - 2 * aa)) * 2 + bb

    def span(j):
        return pl.ds(j * rows, rows)

    fetch = pltpu.make_async_copy(kernels_in, plane_kernels, fetch_s)
    fetch.start()
    barrier = pltpu.get_barrier_semaphore()
    for step in range(1, 2 * n):
        spot = (me * 2 + g + step) % (2 * n)
        pl.semaphore_signal(barrier, inc=1, device_id={"gx": spot // 2, "gy": spot % 2}, device_id_type=MESH)

    rw = jnp.broadcast_to(row_weights[...].astype(jnp.float32), (chans, chans))
    rw = jnp.sum(rw * identity(chans), axis=1, keepdims=True)
    group = 4 if rows % 4 == 0 else 2

    def yz_terms(step, carry):
        for k in range(group):
            y = step * group + k
            part[y] = (feature_row(y) * rw).astype(bf)
        return carry

    lax.fori_loop(0, count // group, yz_terms, 0)
    pl.semaphore_wait(barrier, 2 * n - 1)

    row_copies = []
    for dx in range(-reach, reach + 1):
        for dg in range(2):
            if dx == 0 and dg == 0:
                continue
            slot = reach - dx
            copy = pltpu.make_async_remote_copy(
                src_ref=rows_in,
                dst_ref=row_slots.at[slot, dg],
                send_sem=row_s.at[slot, dg],
                recv_sem=row_r.at[slot, dg],
                device_id={"gx": jnp.clip(me + dx, 0, n - 1), "gy": (g + dg) % 2},
                device_id_type=MESH,
            )
            row_copies.append((dx, copy))

    sub = rows // cuts
    far = sorted([d for d in range(1 - m, m) if d != 0], key=lambda d: -abs(d))
    near = far[::-1]
    partner = a * 2 + 1 - b

    def valid(d):
        return (a + d >= 0) & (a + d < m)

    def spot(d):
        return jnp.clip(a + d, 0, m - 1)

    def sub_span(j, h):
        return pl.ds(j * rows + h * sub, sub)

    pair_copies = {}
    line_copies = {}
    for d in far + [0]:
        for h in range(cuts):
            pair_copies[d, h] = pltpu.make_async_remote_copy(
                src_ref=part.at[sub_span(piece(1 - b, spot(d)), h)],
                dst_ref=pair_in.at[d + m - 1, h],
                send_sem=pair_s.at[d + m - 1, h],
                recv_sem=pair_r.at[d + m - 1, h],
                device_id={"gx": partner},
                device_id_type=MESH,
            )
            if d != 0:
                line_copies[d, h] = pltpu.make_async_remote_copy(
                    src_ref=pair_sum.at[d + m - 1, h],
                    dst_ref=line_in.at[d + m - 1, h],
                    send_sem=line_s.at[d + m - 1, h],
                    recv_sem=line_r.at[d + m - 1, h],
                    device_id={"gx": spot(d) * 2 + b},
                    device_id_type=MESH,
                )
    for (d, h), copy in pair_copies.items():
        pl.when(valid(d))(copy.start)
    for d in far:
        for h in range(cuts):

            @pl.when(valid(d))
            def _():
                pair_copies[d, h].wait_recv()
                mine = part[sub_span(piece(b, spot(d)), h)].astype(jnp.float32)
                pair_sum[d + m - 1, h] = (mine + pair_in[d + m - 1, h].astype(jnp.float32)).astype(bf)
                line_copies[d, h].start()

    fetch.wait()
    turned[...] = flipped(column_weights[...])
    wide[...] = flipped(expand[...]).astype(bf)
    for p in range(plane_kernels.shape[0]):
        for layer in range(2):
            for off in range(3):
                taps = plane_kernels[p, layer, :, off].reshape(3 * chans, chans)
                weights[p, layer, off * chans : (off + 1) * chans, :] = flipped(taps).astype(bf)

    row_sums[...] = jnp.zeros(row_sums.shape, jnp.float32)
    depth = depth_weights[...].astype(jnp.float32)
    lane = lax.broadcasted_iota(jnp.int32, (chans, cols), 1)

    def row_terms(step, carry):
        xy, xz = row_sums[0], row_sums[1]
        for k in range(group):
            y = step * group + k
            f = feature_row(y)
            xy = jnp.where(lane == g * count + y, jnp.sum(f * depth, axis=1, keepdims=True), xy)
            xz = xz + f * column(turned[...], y)
        row_sums[0] = xy
        row_sums[1] = xz
        return carry

    lax.fori_loop(0, count // group, row_terms, 0)
    rows_in[...] = row_sums[...].astype(bf)
    mine_at = piece(b, a)
    for h in range(cuts):
        at = pl.ds(h * sub, sub)
        pair_copies[0, h].wait_recv()
        mine = part[sub_span(mine_at, h)].astype(jnp.float32)
        yz_sum[at] = mine + pair_in[m - 1, h].astype(jnp.float32)
    for d in near:
        for h in range(cuts):

            @pl.when(valid(-d))
            def _():
                at = pl.ds(h * sub, sub)
                line_copies[d, h].wait_recv()
                yz_sum[at] = yz_sum[at] + line_in[d + m - 1, h].astype(jnp.float32)

    yz_plane[pl.ds(reach * chans, rows * chans), :] = yz_sum[...].astype(bf).reshape(rows * chans, cols)

    place = g * n + mine_at
    last = 2 * n - 1
    edge = reach * chans
    before = jnp.maximum(place - 1, 0)
    after = jnp.minimum(place + 1, last)
    up = pltpu.make_async_remote_copy(
        src_ref=yz_plane.at[pl.ds(edge, edge)],
        dst_ref=yz_plane.at[pl.ds(edge + rows * chans, edge)],
        send_sem=halo_s.at[0],
        recv_sem=halo_r.at[0],
        device_id={"gx": owner(before % n), "gy": before // n},
        device_id_type=MESH,
    )
    down = pltpu.make_async_remote_copy(
        src_ref=yz_plane.at[pl.ds(rows * chans, edge)],
        dst_ref=yz_plane.at[pl.ds(0, edge)],
        send_sem=halo_s.at[1],
        recv_sem=halo_r.at[1],
        device_id={"gx": owner(after % n), "gy": after // n},
        device_id_type=MESH,
    )
    pl.when(place > 0)(up.start)
    pl.when(place < last)(down.start)
    for dx, copy in row_copies:
        pl.when((me + dx >= 0) & (me + dx < n))(copy.start)

    @pl.when(place == 0)
    def _():
        yz_plane[pl.ds(0, edge), :] = jnp.zeros((edge, cols), jnp.bfloat16)

    @pl.when(place == last)
    def _():
        yz_plane[pl.ds(edge + rows * chans, edge), :] = jnp.zeros((edge, cols), jnp.bfloat16)

    def inner_row(i, keep):
        window = yz_plane[pl.ds(pl.multiple_of(i * chans, chans), 3 * chans), :]
        inner = silu(conv_row(window, weights[2, 0])) * keep
        yz_inner[pl.ds(pl.multiple_of(i * chans, chans), chans), :] = inner.astype(jnp.bfloat16)

    for i in range(reach, rows):
        inner_row(i, 1.0)
    pl.when(place < last)(up.wait_recv)
    pl.when(place > 0)(down.wait_recv)
    for i in list(range(reach)) + list(range(rows, rows + 2)):
        keep = 1.0
        if i == 0:
            keep = (place > 0).astype(jnp.float32)
        if i == rows + 1:
            keep = (place < last).astype(jnp.float32)
        inner_row(i, keep)
    def give(j, h, sems, at, target):
        return pltpu.make_async_remote_copy(
            src_ref=yz_out.at[sub_span(j, h)],
            dst_ref=yz_out.at[sub_span(j, h)],
            send_sem=sems[0].at[at, h],
            recv_sem=sems[1].at[at, h],
            device_id={"gx": target},
            device_id_type=MESH,
        )

    spread = (spread_s, spread_r)
    cross = (cross_s, cross_r)
    sends = []
    for h in range(cuts):
        for r in range(h * sub, (h + 1) * sub):
            done = conv_row(yz_inner[pl.ds(r * chans, 3 * chans), :], weights[2, 1])
            yz_out[mine_at * rows + r] = done.astype(bf)
        for d in near:
            copy = give(mine_at, h, spread, d + m - 1, spot(d) * 2 + b)
            pl.when(valid(d))(copy.start)
            sends.append((d, copy))
        copy = give(mine_at, h, cross, m - 1, partner)
        copy.start()
        sends.append((0, copy))

    for dx, copy in row_copies:
        pl.when((me - dx >= 0) & (me - dx < n))(copy.wait_recv)
    planes = rows_in.shape[0]
    for s in range(2 * reach + 1):
        at = me + s - reach
        inside = (at >= 0) & (at < n)
        here = pl.ds(s * chans, chans)

        @pl.when(inside)
        def _():
            first = rows_in[...] if s == reach else row_slots[s, 0]
            total = first.astype(jnp.float32) + row_slots[s, 1].astype(jnp.float32)
            row_plane[:, here, :] = total.astype(jnp.bfloat16)

        @pl.when(jnp.logical_not(inside))
        def _():
            row_plane[:, here, :] = jnp.zeros((planes, chans, cols), jnp.bfloat16)

    for p in range(planes):
        for s in range(3):
            at = me + s - 1
            keep = ((at >= 0) & (at < n)).astype(jnp.float32)
            inner = silu(conv_row(row_plane[p, s * chans : (s + 3) * chans, :], weights[p, 0]))
            row_inner[p, s * chans : (s + 1) * chans, :] = (inner * keep).astype(jnp.bfloat16)
    xy_out[...] = conv_row(row_inner[0], weights[0, 1]).astype(bf).astype(jnp.float32)
    xz_out[...] = conv_row(row_inner[1], weights[1, 1]).astype(bf).astype(jnp.float32)

    step_rows = 4 if sub % 4 == 0 else (2 if sub % 2 == 0 else 1)

    def finish(j, h):
        def some_rows(step, carry):
            at = [j * rows + h * sub + step * step_rows + k for k in range(step_rows)]
            mixed = []
            for y in at:
                product = column(xy_out[...], g * count + y) * xz_out[...]
                product = product * yz_out[y].astype(jnp.float32)
                mixed.append((product_scale * product).astype(bf))
            mixed = jnp.concatenate(mixed, axis=1)
            hidden = silu(jnp.dot(wide[...], mixed, preferred_element_type=jnp.float32)).astype(bf)
            branch = jnp.dot(shrink[...], hidden, preferred_element_type=jnp.float32)
            for k, y in enumerate(at):
                updated[y] = (feature_row(y) + branch[:, k * cols : (k + 1) * cols]).astype(bf)
            return carry

        lax.fori_loop(0, sub // step_rows, some_rows, 0)

    for h in range(cuts):
        finish(mine_at, h)
    for h in range(cuts):
        for d in near:

            @pl.when(valid(d))
            def _():
                j = piece(b, spot(d))
                give(j, h, spread, m - 1 - d, partner).wait_recv()
                give(j, h, cross, m - 1 + d, partner).start()
                finish(j, h)

    for h in range(cuts):
        for d in [0] + near:

            @pl.when(valid(d))
            def _():
                j = piece(1 - b, spot(d))
                give(j, h, cross, m - 1 + d, partner).wait_recv()
                finish(j, h)

    for d in near:
        for h in range(cuts):
            pl.when(valid(d))(give(piece(b, spot(d)), h, cross, m - 1 + d, partner).wait_send)
    for d, copy in sends:
        pl.when(valid(d))(copy.wait_send)
    for (d, h), copy in list(pair_copies.items()) + list(line_copies.items()):
        pl.when(valid(d))(copy.wait_send)
    for dx, copy in row_copies:
        pl.when((me + dx >= 0) & (me + dx < n))(copy.wait_send)
    pl.when(place > 0)(up.wait_send)
    pl.when(place < last)(down.wait_send)


def fused(voxels, occupancy, row_weights, column_weights, depth_weights, plane_kernels, expand_weight, shrink_weight):
    n = lax.axis_size("gx")
    m = n // 2
    count, cols, chans = voxels.shape[1:]
    rows = count // n
    sets, layers = plane_kernels.shape[:2]
    planes = 2
    span = 2 * reach + 1
    bf = jnp.bfloat16
    f32 = jnp.float32
    dma = pltpu.SemaphoreType.DMA
    block = dma((2 * m - 1, cuts))
    updated = pl.pallas_call(
        functools.partial(block_kernel, n),
        out_shape=pltpu.VMEM((count, chans, cols), bf),
        in_specs=[pl.BlockSpec(memory_space=pl.ANY if k == 5 else pltpu.VMEM) for k in range(8)],
        out_specs=pl.BlockSpec(memory_space=pltpu.VMEM),
        scratch_shapes=[
            pltpu.VMEM(plane_kernels.shape, bf),
            dma,
            pltpu.VMEM((count, chans, cols), bf),
            pltpu.VMEM((planes, chans, cols), bf),
            pltpu.VMEM((sets, layers, 3 * chans, 3 * chans), bf),
            pltpu.VMEM(expand_weight.shape[::-1], bf),
            pltpu.VMEM((count, chans, cols), bf),
            pltpu.VMEM((chans, 2 * count), f32),
            pltpu.VMEM((chans, cols), f32),
            pltpu.VMEM((planes, chans, cols), f32),
            pltpu.VMEM((chans, count), f32),
            pltpu.VMEM((2 * m - 1, cuts, rows // cuts, chans, cols), bf),
            pltpu.VMEM((2 * m - 1, cuts, rows // cuts, chans, cols), bf),
            pltpu.VMEM((2 * m - 1, cuts, rows // cuts, chans, cols), bf),
            pltpu.VMEM((rows, chans, cols), f32),
            pltpu.VMEM(((rows + 4) * chans, cols), bf),
            pltpu.VMEM(((rows + 2) * chans, cols), bf),
            pltpu.VMEM((span, 2, planes, chans, cols), bf),
            pltpu.VMEM((planes, span * chans, cols), bf),
            pltpu.VMEM((planes, 3 * chans, cols), bf),
            block, block, block, block, dma((2,)), dma((2,)),
            dma((span, 2)), dma((span, 2)), block, block, block, block,
        ],
        compiler_params=pltpu.CompilerParams(collective_id=0, has_side_effects=True),
    )(
        voxels[0].transpose(0, 2, 1),
        occupancy[0],
        row_weights,
        column_weights,
        depth_weights.T,
        plane_kernels,
        expand_weight,
        shrink_weight.T,
    )
    return updated.transpose(0, 2, 1)[None]


def fits(voxels):
    n = lax.axis_size("gx")
    sides = lax.axis_size("gy")
    xs, ys, zs, _ = voxels.shape
    return xs == 1 and sides == 2 and n % 2 == 0 and n >= 4 and ys % n == 0 and ys // n >= reach and ys // n % cuts == 0 and 2 * ys == zs


def plain_planes(features, row_weights, column_weights, depth_weights, plane_kernels):
    xy_plane = jnp.einsum(
        "xyzc,zc->xyc", features, depth_weights, preferred_element_type=jnp.float32
    ).astype(jnp.bfloat16)
    xz_part = jnp.einsum(
        "xyzc,yc->xzc", features, column_weights, preferred_element_type=jnp.float32
    )
    yz_part = jnp.einsum("xyzc,xc->yzc", features, row_weights, preferred_element_type=jnp.float32)
    xy_out = plane_block(xy_plane, plane_kernels[0], rim_xy)
    xz_plane = lax.psum(xz_part, "gy").astype(jnp.bfloat16)
    xz_out = plane_block(xz_plane, plane_kernels[1], rim_xz)
    yz_plane = lax.psum(yz_part, "gx").astype(jnp.bfloat16)
    yz_out = plane_block(yz_plane, plane_kernels[2], rim_yz)
    return xy_out, xz_out, yz_out


def shards(
    voxels,
    occupancy,
    row_weights,
    column_weights,
    depth_weights,
    plane_kernels,
    expand_weight,
    shrink_weight,
):
    if fits(voxels):
        return fused(
            voxels,
            occupancy,
            row_weights,
            column_weights,
            depth_weights,
            plane_kernels,
            expand_weight,
            shrink_weight,
        )
    features = voxels * occupancy.astype(jnp.bfloat16)[..., None]
    xy_out, xz_out, yz_out = plain_planes(features, row_weights, column_weights, depth_weights, plane_kernels)
    product = xy_out.astype(jnp.float32)[:, :, None, :] * xz_out.astype(jnp.float32)[:, None, :, :]
    product = product * yz_out.astype(jnp.float32)[None, :, :, :]
    mixed = (product_scale * product).astype(jnp.bfloat16)
    hidden = jax.nn.silu(
        jnp.einsum("xyzc,ch->xyzh", mixed, expand_weight, preferred_element_type=jnp.float32)
    ).astype(jnp.bfloat16)
    branch = jnp.einsum("xyzh,hc->xyzc", hidden, shrink_weight, preferred_element_type=jnp.float32)
    return (features.astype(jnp.float32) + branch).astype(jnp.bfloat16)


def solution(mesh):
    in_specs = (
        P(("groups", "gx"), "gy", None, None),
        P(("groups", "gx"), "gy", None),
        P("gx", None),
        P("gy", None),
        P(),
        P(),
        P(),
        P(),
    )
    out_specs = P(("groups", "gx"), "gy", None, None)
    return jax.shard_map(shards, mesh=mesh, in_specs=in_specs, out_specs=out_specs, check_vma=False)
```

profile of v0, /device:TPU:0, one launch (start us, length us, event | category | flops | bytes accessed | tf_op | source)
XLA Modules:
  0.0 46.4 jit_solution(915742447559301888)
XLA Ops:
  0.0 45.5 %shard_map.82 = bf16[64,64,128]{2,1,0:T(8,128)(2,1)S(1)} custom-call(bf16[64,64,128]{2,1,0:T(8,128)(2,1)} %bitcast.10, s32[64,128]{1,0:T(8,128)} %bitcast.11, bf16[1,64]{1,0:T(2,128)(2,1)} %row_weights.1, bf16[64,64]{1,0:T(8,128)(2,1)} %column_weights.1, bf16[64,128]{1,0:T(8,128)(2,1)} %bitcast.12, bf16[3,2,3,3,64,64]{5,4,3,2,1,0:T(8,128)(2,1)} %kernels_in.1, ...), custom_call_target="tpu_custom_call" | custom-call | tf_op jit(solution)/shard_map/pallas_call | solution.py:421
  45.5 1.0 %copy.10 = bf16[1,64,128,64]{2,3,1,0:T(8,128)(2,1)} copy(bf16[1,64,128,64]{2,3,1,0:T(8,128)(2,1)S(1)} %bitcast.9) | data formatting | bytes 2097152
where the time goes:
time: 46.6 us; the launch traced here: 46.4 us
  Pallas kernels  45.5 us (98%)
  local copies, waits for them, and re-layouts  0.97 us (2%)
    pallas_call x1, Pallas kernels, fused(): pl.pallas_call(functools.partial(block_kernel, n), out_shape=pltpu.VMEM((...  45.5 us
    unnamed x1, local copies, waits for them, and re-layouts  0.97 us

commit v1 on v0

v1 whole, which is shorter than its diff:
```python
import functools

import jax
import jax.numpy as jnp
from jax import lax
from jax.experimental import pallas as pl
from jax.experimental.pallas import tpu as pltpu
from jax.sharding import PartitionSpec as P

MESH = pl.DeviceIdType.MESH
reach = 2

product_scale = 8.0


def with_halo(cells, sides, width):
    for axis, dim in sides:
        count = lax.axis_size(axis)
        ends = count - 1
        head = lax.slice_in_dim(cells, 0, width, axis=dim)
        tail = lax.slice_in_dim(cells, cells.shape[dim] - width, cells.shape[dim], axis=dim)
        cells = jnp.concatenate(
            [
                lax.ppermute(tail, axis, [(i, (i + 1) % count) for i in range(ends)]),
                cells,
                lax.ppermute(head, axis, [((i + 1) % count, i) for i in range(ends)]),
            ],
            axis=dim,
        )
    return cells


def conv_valid(padded, kernel):
    rows = padded.shape[0] - 2
    cols = padded.shape[1] - 2
    total = jnp.zeros((rows, cols, kernel.shape[-1]), jnp.float32)
    for row_off in range(3):
        for col_off in range(3):
            window = padded[row_off : row_off + rows, col_off : col_off + cols]
            total = total + jnp.einsum(
                "ijc,co->ijo", window, kernel[row_off, col_off], preferred_element_type=jnp.float32
            )
    return total


def plane_block(plane, kernels, extend):
    inner = jax.nn.silu(conv_valid(extend(plane), kernels[0])).astype(jnp.bfloat16)
    return conv_valid(extend(inner), kernels[1]).astype(jnp.bfloat16)


def rim_xy(plane):
    return with_halo(plane, (("gx", 0), ("gy", 1)), 1)


def rim_xz(plane):
    padded = with_halo(plane, (("gx", 0),), 1)
    return jnp.pad(padded, ((0, 0), (1, 1), (0, 0)))


def rim_yz(plane):
    padded = with_halo(plane, (("gy", 0),), 1)
    return jnp.pad(padded, ((0, 0), (1, 1), (0, 0)))


def conv_row(window, weight):
    taps = jnp.dot(weight, window, preferred_element_type=jnp.float32)
    chans = taps.shape[0] // 3
    cols = taps.shape[1]
    lane = lax.broadcasted_iota(jnp.int32, (chans, cols), 1)
    left = pltpu.roll(taps[:chans], 1, 1)
    right = pltpu.roll(taps[2 * chans :], cols - 1, 1)
    left = jnp.where(lane == 0, 0.0, left)
    right = jnp.where(lane == cols - 1, 0.0, right)
    return taps[chans : 2 * chans] + left + right


def silu(v):
    half = 0.5 * v
    return half + half * jnp.tanh(half)


def identity(size):
    row = lax.broadcasted_iota(jnp.int32, (size, size), 0)
    col = lax.broadcasted_iota(jnp.int32, (size, size), 1)
    return jnp.where(row == col, 1.0, 0.0)


def flipped(x):
    eye = identity(x.shape[1]).astype(x.dtype)
    return lax.dot_general(eye, x, (((1,), (1,)), ((), ())), preferred_element_type=jnp.float32)


def column(x, at):
    lane = lax.broadcasted_iota(jnp.int32, x.shape, 1)
    return jnp.sum(jnp.where(lane == at, x, 0.0), axis=1, keepdims=True)


def pick(index, values):
    chosen = values[0]
    for i, value in enumerate(values):
        if i > 0 and value != values[0]:
            chosen = jnp.where(index == i, value, chosen)
    return chosen


def others(m, z):
    return [k for k in range(m) if k != z]


def joined(m, z, k):
    return z in (0, m - 1) and abs(k - z) == 2


def joins(m, z):
    found = []
    for end, step in ((0, 1), (m - 1, -1)):
        if z == end + step:
            found.append((end, z + step))
    return found


def sum_order(m, z):
    first = {k for _, k in joins(m, z)} | {k for k in others(m, z) if joined(m, z, k)}
    ks = sorted(others(m, z), key=lambda k: (k not in first, -abs(k - z)))
    rest = ks[1:]
    chunks = [(ks[0], 0), (ks[0], 1)] + [(k, 0) for k in rest] + [(k, 1) for k in rest] + [(z, 0), (z, 1)]
    return [2 * k + h for k, h in chunks]


def passed(m, z, k):
    return k in (0, m - 1) and abs(k - z) == 2


def give_order(m, z):
    return sorted(others(m, z), key=lambda k: -abs(k - z))


def take_order(m, z):
    direct = sorted([k for k in others(m, z) if not passed(m, k, z)], key=lambda k: (k in (0, m - 1), -abs(k - z)))
    late = [k for k in others(m, z) if passed(m, k, z)]
    ks = direct + late
    chunks = [(k, h) for k in ks[:2] for h in (1,)] + [(k, 0) for k in ks[:2]] + [(k, h) for k in ks[2:] for h in (1, 0)]
    return [2 * k + h for k, h in chunks]


def block_kernel(
    n, voxels_in, occupancy_in, row_weights_in, column_weights_in, depth_in, kernels_in, expand_in, shrink_in, updated,
    voxels, occupancy, row_weights, column_weights, depth_weights, plane_kernels, expand, shrink, load_s, fetch_s,
    part, rows_in, weights, wide, yz_out, row_sums, turned,
    pair_in, pair_sum, line_in, yz_sum, yz_plane, yz_inner,
    row_other, row_slots, row_plane, row_inner, outs,
    pair_s, pair_r, line_s, line_r, halo_s, halo_r, row_s, row_r, core_s, core_r, spread_s, spread_r, cross_s, cross_r, known,
):
    me = lax.axis_index("gx")
    g = lax.axis_index("gy")
    m = n // 2
    a = me // 2
    b = me % 2
    count, chans, cols = part.shape
    rows = count // n
    sub = 2 * reach
    bf = jnp.bfloat16
    f32 = jnp.float32
    partner = a * 2 + 1 - b

    def table(make):
        return [make(z) for z in range(m)]

    def feature_row(y):
        return voxels[y].astype(f32) * occupancy[pl.ds(y, 1), :].astype(f32)

    def piece(bb, aa):
        return bb * m + aa + bb * (m - 1 - 2 * aa)

    def owner(j):
        bb = j // m
        aa = j % m
        return (aa + bb * (m - 1 - 2 * aa)) * 2 + bb

    def offset(h, r):
        edge = r if r < reach else rows - sub + r
        if isinstance(h, int):
            return edge if h == 0 else reach + r
        return jnp.where(h == 0, edge, reach + r)

    def chunk(bb, q):
        return pl.ds(piece(bb, q // 2) * rows + (q % 2) * sub, sub)

    def remote(src, dst, send, recv, gx, gy=None):
        target = {"gx": gx} if gy is None else {"gx": gx, "gy": gy}
        return pltpu.make_async_remote_copy(
            src_ref=src, dst_ref=dst, send_sem=send, recv_sem=recv, device_id=target, device_id_type=MESH
        )

    place = g * n + piece(b, a)
    last = 2 * n - 1
    before = jnp.maximum(place - 1, 0)
    after = jnp.minimum(place + 1, last)

    barrier = pltpu.get_barrier_semaphore()

    def greet(gx, gy):
        pl.semaphore_signal(barrier, inc=1, device_id={"gx": gx, "gy": gy}, device_id_type=MESH)

    lower = a > 0
    upper = a < m - 1
    slant = jnp.where(b == 0, lower, upper)
    seam_low = place == n - 1
    seam_high = place == n
    greet(partner, g)
    greet(me, 1 - g)
    pl.when(lower)(lambda: greet(jnp.maximum(me - 2, 0), g))
    pl.when(upper)(lambda: greet(jnp.minimum(me + 2, n - 1), g))
    pl.when(slant)(lambda: greet(jnp.clip(me + 2 * b - 1, 0, n - 1), g))
    pl.when(seam_low)(lambda: greet(owner(0), 1 - g))
    pl.when(seam_high)(lambda: greet(owner(n - 1), 1 - g))
    greeters = (
        2 + lower.astype(jnp.int32) + upper.astype(jnp.int32) + slant.astype(jnp.int32)
        + seam_low.astype(jnp.int32) + seam_high.astype(jnp.int32)
    )

    order = table(lambda z: sum_order(m, z))
    turns = [pick(a, [o[i] for o in order]) for i in range(2 * m)]
    lanes = [pick(a, [sum_order(m, z)[i] // 2 for z in range(m)]) for i in (0, 2)]
    lanes += [pick(a, [sum_order(m, z)[2 + i] // 2 for z in range(m)]) for i in range(1, m - 2)]
    lanes = lanes + [a]

    small = [
        pltpu.make_async_copy(row_weights_in, row_weights, load_s.at[0]),
        pltpu.make_async_copy(occupancy_in, occupancy, load_s.at[1]),
    ]
    large = []
    for bb in (1 - b, b):
        for k in lanes:
            at = pl.ds(piece(bb, k) * rows, rows)
            large.append(pltpu.make_async_copy(voxels_in.at[at], voxels.at[at], load_s.at[2 + len(large)]))
    fetches = [
        pltpu.make_async_copy(kernels_in, plane_kernels, fetch_s.at[0]),
        pltpu.make_async_copy(column_weights_in, column_weights, fetch_s.at[1]),
        pltpu.make_async_copy(depth_in, depth_weights, fetch_s.at[2]),
        pltpu.make_async_copy(expand_in, expand, fetch_s.at[3]),
        pltpu.make_async_copy(shrink_in, shrink, fetch_s.at[4]),
    ]
    for copy in small + large + fetches:
        copy.start()

    for copy in small:
        copy.wait()
    rw = jnp.broadcast_to(row_weights[...].astype(f32), (chans, chans))
    rw = jnp.sum(rw * identity(chans), axis=1, keepdims=True)

    def yz_terms(j):
        for h in range(2):
            for r in range(sub):
                part[j * rows + h * sub + r] = (feature_row(j * rows + offset(h, r)) * rw).astype(bf)

    pair_copies = []
    for q in turns:
        pair_copies.append(remote(part.at[chunk(1 - b, q)], pair_in.at[q], pair_s.at[q], pair_r.at[q], partner))

    large[0].wait()
    yz_terms(piece(1 - b, lanes[0]))
    pl.semaphore_wait(barrier, greeters)
    pair_copies[0].start()
    pair_copies[1].start()
    for i in range(1, m - 1):
        large[i].wait()
        yz_terms(piece(1 - b, lanes[i]))
        pair_copies[1 + i].start()
    for i in range(1, m - 1):
        pair_copies[m - 1 + i].start()
    large[m - 1].wait()
    yz_terms(piece(1 - b, lanes[m - 1]))
    pair_copies[2 * m - 2].start()
    pair_copies[2 * m - 1].start()

    def tell(level, side):
        step = 2 if side == 0 else -2
        pl.semaphore_signal(
            known.at[level, side], inc=1, device_id={"gx": jnp.clip(me - step, 0, n - 1), "gy": g}, device_id_type=MESH
        )

    def heard(level, side):
        return (a + level <= m - 1) if side == 0 else (a - level >= 0)

    def tells(level, side):
        return (lower if side == 0 else upper) & heard(level - 1, side)

    def tell_level(level):
        for side in range(2):
            if level > 2:
                pl.when(heard(level - 1, side))(lambda: pl.semaphore_wait(known.at[level - 1, side], 1))
            if level < m:
                pl.when(tells(level, side))(lambda: tell(level, side))

    tell_level(2)

    for i in range(m):
        large[m + i].wait()
        yz_terms(piece(b, lanes[i]))

    for copy in fetches:
        copy.wait()
    turned[...] = flipped(column_weights[...])
    row_sums[...] = jnp.zeros(row_sums.shape, f32)
    lane = lax.broadcasted_iota(jnp.int32, (chans, cols), 1)

    group = 4
    share = count // (2 * m)

    def row_terms(first):
        depth = depth_weights[...].astype(f32)

        def some(step, carry):
            xy, xz = row_sums[0], row_sums[1]
            for k in range(group):
                y = first + step * group + k
                f = feature_row(y)
                xy = jnp.where(lane == g * count + y, jnp.sum(f * depth, axis=1, keepdims=True), xy)
                xz = xz + f * column(turned[...], y)
            row_sums[0] = xy
            row_sums[1] = xz
            return carry

        lax.fori_loop(0, share // group, some, 0)

    def flip_plane(p, layer):
        for off in range(3):
            taps = plane_kernels[p, layer, :, off].reshape(3 * chans, chans)
            weights[p, layer, off * chans : (off + 1) * chans, :] = flipped(taps).astype(bf)

    for level in range(3, m):
        tell_level(level)

    holds = table(lambda z: [k for _, k in joins(m, z)])
    held = pick(a, [ks[0] if ks else -1 for ks in holds])
    source = pick(a, [joins(m, z)[0][0] if joins(m, z) else -1 for z in range(m)])

    def line_target(i):
        k = turns[i] // 2
        gx = pick(a, [((z + (1 if order[z][i] // 2 > z else -1)) if joined(m, z, order[z][i] // 2) else order[z][i] // 2) for z in range(m)])
        slot = pick(a, [2 * (m if joined(m, z, order[z][i] // 2) else z) + order[z][i] % 2 for z in range(m)])
        return k, gx * 2 + b, slot

    line_copies = []
    for i in range(2 * m - 2):
        k, gx, slot = line_target(i)
        q = turns[i]
        line_copies.append(remote(pair_sum.at[q], line_in.at[slot], line_s.at[q], line_r.at[slot], gx))

    def reduce_pair(i):
        q = turns[i]
        pair_copies[i].wait_recv()
        mine = part[chunk(b, q)].astype(f32)
        pair_sum[q] = (mine + pair_in[q].astype(f32)).astype(bf)
        pl.when(q // 2 != held)(line_copies[i].start)

    def reduce_joined(h):
        @pl.when(held >= 0)
        def _():
            q = 2 * jnp.maximum(held, 0) + h
            slot = 2 * m + h
            remote(pair_sum.at[q], line_in.at[slot], line_s.at[q], line_r.at[slot], partner).wait_recv()
            pair_sum[q] = (pair_sum[q].astype(f32) + line_in[slot].astype(f32)).astype(bf)
            line_copies[h].start()

    def reduce_own(h):
        q = turns[2 * m - 2 + h]
        pair_copies[2 * m - 2 + h].wait_recv()
        yz_sum[h] = part[chunk(b, q)].astype(f32) + pair_in[q].astype(f32)

    def reduce_line(h):
        for i in range(m - 1):
            src = pick(a, [sorted(others(m, z), key=lambda s: (abs(s - z), s))[i] for z in range(m)])
            skip = pick(a, [int(joined(m, sorted(others(m, z), key=lambda s: (abs(s - z), s))[i], z)) for z in range(m)])

            @pl.when(skip == 0)
            def _():
                slot = 2 * src + h
                remote(pair_sum.at[slot], line_in.at[slot], line_s.at[slot], line_r.at[slot], partner).wait_recv()
                yz_sum[h] = yz_sum[h] + line_in[slot].astype(f32)

    row_terms(0)
    reduce_pair(0)
    row_terms(share)
    reduce_pair(1)
    tell_level(m)
    row_terms(2 * share)
    reduce_pair(2)
    wide[...] = flipped(expand[...]).astype(bf)
    flip_plane(2, 0)
    reduce_joined(0)
    for i in range(3, 2 * m - 2):
        row_terms(i * share)
        reduce_pair(i)
        if i == 3:
            flip_plane(2, 1)
            reduce_joined(1)
    for i in range(2 * m - 2, 2 * m):
        row_terms(i * share)
    rows_in[...] = row_sums[...].astype(bf)
    core = remote(rows_in.at[1 - g], row_other.at[...], core_s.at[0], core_r.at[0], me, 1 - g)
    core.start()
    for layer in range(2):
        flip_plane(g, layer)

    edge = reach * chans
    halo = [
        (place > 0, place < last, remote(
            yz_plane.at[pl.ds(edge, edge)], yz_plane.at[pl.ds(edge + rows * chans, edge)],
            halo_s.at[0], halo_r.at[0], owner(before % n), before // n,
        )),
        (place < last, place > 0, remote(
            yz_plane.at[pl.ds(rows * chans, edge)], yz_plane.at[pl.ds(0, edge)],
            halo_s.at[1], halo_r.at[1], owner(after % n), after // n,
        )),
    ]

    @pl.when(place == 0)
    def _():
        yz_plane[pl.ds(0, edge), :] = jnp.zeros((edge, cols), bf)

    @pl.when(place == last)
    def _():
        yz_plane[pl.ds(edge + rows * chans, edge), :] = jnp.zeros((edge, cols), bf)

    def settle(h):
        for r in range(sub):
            at = (reach + offset(h, r)) * chans
            yz_plane[at : at + chans, :] = yz_sum[h, r].astype(bf)

    reduce_own(0)
    core.wait_recv()
    mid = rows_in[g].astype(f32) + row_other[...].astype(f32)
    row_slots[reach] = mid.astype(bf)
    row_copies = []
    for dx in range(-reach, reach + 1):
        if dx != 0:
            slot = reach - dx
            copy = remote(
                row_slots.at[reach], row_slots.at[slot], row_s.at[slot], row_r.at[slot], jnp.clip(me + dx, 0, n - 1)
            )
            row_copies.append((dx, copy))
    reduce_line(0)
    settle(0)
    for sends, _, copy in halo:
        pl.when(sends)(copy.start)
    for dx, copy in row_copies:
        pl.when((me + dx >= 0) & (me + dx < n))(copy.start)
    reduce_own(1)
    reduce_line(1)
    settle(1)

    def inner_row(i, keep):
        inner = silu(conv_row(yz_plane[i * chans : (i + 3) * chans, :], weights[2, 0])) * keep
        yz_inner[i * chans : (i + 1) * chans, :] = inner.astype(bf)

    spread_copies = []
    own = piece(b, a)

    def give_chunk(h):
        for r in range(sub):
            at = offset(h, r) * chans
            done = conv_row(yz_inner[at : at + 3 * chans, :], weights[2, 1])
            yz_out[own * rows + h * sub + r] = done.astype(bf)
        q = 2 * a + h
        cross_copy(b, q).start()
        for i in range(m - 1):
            k = pick(a, [give_order(m, z)[i] for z in range(m)])
            skip = pick(a, [int(passed(m, z, give_order(m, z)[i])) for z in range(m)])
            at = chunk(b, q)
            copy = remote(yz_out.at[at], yz_out.at[at], spread_s.at[2 * i + h], spread_r.at[q], k * 2 + b)
            pl.when(skip == 0)(copy.start)
            spread_copies.append((skip == 0, copy))

    def cross_copy(bb, q):
        at = chunk(bb, q)
        return remote(yz_out.at[at], yz_out.at[at], cross_s.at[q], cross_r.at[q], partner)

    for i in range(reach, rows):
        inner_row(i, 1.0)
    give_chunk(1)
    for _, receives, copy in halo:
        pl.when(receives)(copy.wait_recv)
    for i in list(range(reach)) + list(range(rows, rows + 2)):
        keep = 1.0
        if i == 0:
            keep = (place > 0).astype(f32)
        if i == rows + 1:
            keep = (place < last).astype(f32)
        inner_row(i, keep)
    give_chunk(0)

    for dx, copy in row_copies:
        pl.when((me - dx >= 0) & (me - dx < n))(copy.wait_recv)
    for s in range(2 * reach + 1):
        at = me + s - reach
        inside = (at >= 0) & (at < n)
        here = pl.ds(s * chans, chans)

        @pl.when(inside)
        def _():
            row_plane[here, :] = row_slots[s]

        @pl.when(jnp.logical_not(inside))
        def _():
            row_plane[here, :] = jnp.zeros((chans, cols), bf)

    for s in range(3):
        at = me + s - 1
        keep = ((at >= 0) & (at < n)).astype(f32)
        inner = silu(conv_row(row_plane[s * chans : (s + 3) * chans, :], weights[g, 0]))
        row_inner[s * chans : (s + 1) * chans, :] = (inner * keep).astype(bf)
    outs[g] = conv_row(row_inner[...], weights[g, 1]).astype(bf)
    share_out = remote(outs.at[g], outs.at[g], core_s.at[1], core_r.at[1], me, 1 - g)
    share_out.start()
    remote(outs.at[1 - g], outs.at[1 - g], core_s.at[1], core_r.at[1], me, 1 - g).wait_recv()

    def finish(bb, q):
        j = piece(bb, q // 2)
        h = q % 2
        xy_out = outs[0].astype(f32)
        xz_out = outs[1].astype(f32)
        at = [(j * rows + h * sub + r, j * rows + offset(h, r)) for r in range(sub)]
        mixed = []
        for s, y in at:
            product = column(xy_out, g * count + y) * xz_out
            product = product * yz_out[s].astype(f32)
            mixed.append((product_scale * product).astype(bf))
        mixed = jnp.concatenate(mixed, axis=1)
        hidden = silu(jnp.dot(wide[...], mixed, preferred_element_type=f32)).astype(bf)
        branch = jnp.dot(shrink[...], hidden, preferred_element_type=f32)
        for k, (s, y) in enumerate(at):
            updated[y] = (feature_row(y) + branch[:, k * cols : (k + 1) * cols]).astype(bf)

    takes = [pick(a, [take_order(m, z)[i] for z in range(m)]) for i in range(2 * m - 2)]
    hands = table(lambda z: [k for k in others(m, z) if any(passed(m, k, t) and abs(z - t) == 1 for t in others(m, z))])
    handed = pick(a, [ks[0] if ks else -1 for ks in hands])
    onward = pick(a, [(0 if z == 1 else m - 1) if hands[z] else 0 for z in range(m)])

    def hand_copy(h):
        q = 2 * jnp.maximum(handed, 0) + h
        at = chunk(b, q)
        return remote(yz_out.at[at], yz_out.at[at], spread_s.at[2 * (m - 1) + h], spread_r.at[q], onward * 2 + b)

    def take(i):
        q = takes[i]
        at = chunk(b, q)
        remote(yz_out.at[at], yz_out.at[at], spread_s.at[0], spread_r.at[q], partner).wait_recv()
        cross_copy(b, q).start()
        for h in range(2):
            pl.when((handed >= 0) & (q == 2 * handed + h))(hand_copy(h).start)
        finish(b, q)

    crossed = [2 * a + 1, 2 * a] + takes

    def take_crossed(i):
        q = crossed[i]
        cross_copy(1 - b, q).wait_recv()
        finish(1 - b, q)

    finish(b, 2 * a + 1)
    finish(b, 2 * a)
    takes_done = 0
    crossed_done = 0
    for step in "tctcttctct" + "c" * 4:
        if step == "t":
            take(takes_done)
            takes_done += 1
        else:
            take_crossed(crossed_done)
            crossed_done += 1
    while takes_done < len(takes):
        take(takes_done)
        takes_done += 1
    while crossed_done < len(crossed):
        take_crossed(crossed_done)
        crossed_done += 1

    for copy in pair_copies:
        copy.wait_send()
    for copy in line_copies:
        copy.wait_send()
    for sends, _, copy in halo:
        pl.when(sends)(copy.wait_send)
    core.wait_send()
    share_out.wait_send()
    for dx, copy in row_copies:
        pl.when((me + dx >= 0) & (me + dx < n))(copy.wait_send)
    for sent, copy in spread_copies:
        pl.when(sent)(copy.wait_send)
    for h in range(2):
        pl.when(handed >= 0)(hand_copy(h).wait_send)
    for q in crossed:
        cross_copy(b, q).wait_send()


def fused(voxels, occupancy, row_weights, column_weights, depth_weights, plane_kernels, expand_weight, shrink_weight):
    n = lax.axis_size("gx")
    m = n // 2
    count, cols, chans = voxels.shape[1:]
    rows = count // n
    sub = 2 * reach
    sets, layers = plane_kernels.shape[:2]
    planes = 2
    span = 2 * reach + 1
    bf = jnp.bfloat16
    f32 = jnp.float32
    dma = pltpu.SemaphoreType.DMA
    operands = (
        voxels[0].transpose(0, 2, 1),
        occupancy[0],
        row_weights,
        column_weights,
        depth_weights.T,
        plane_kernels,
        expand_weight,
        shrink_weight.T,
    )
    updated = pl.pallas_call(
        functools.partial(block_kernel, n),
        out_shape=pltpu.VMEM((count, chans, cols), bf),
        in_specs=[pl.BlockSpec(memory_space=pl.ANY) for _ in operands],
        out_specs=pl.BlockSpec(memory_space=pltpu.VMEM),
        scratch_shapes=[pltpu.VMEM(x.shape, x.dtype) for x in operands]
        + [
            dma((2 + 2 * m,)),
            dma((5,)),
            pltpu.VMEM((count, chans, cols), bf),
            pltpu.VMEM((planes, chans, cols), bf),
            pltpu.VMEM((sets, layers, 3 * chans, 3 * chans), bf),
            pltpu.VMEM(expand_weight.shape[::-1], bf),
            pltpu.VMEM((count, chans, cols), bf),
            pltpu.VMEM((planes, chans, cols), f32),
            pltpu.VMEM((chans, count), f32),
            pltpu.VMEM((2 * m, sub, chans, cols), bf),
            pltpu.VMEM((2 * m, sub, chans, cols), bf),
            pltpu.VMEM((2 * m + 2, sub, chans, cols), bf),
            pltpu.VMEM((2, sub, chans, cols), f32),
            pltpu.VMEM(((rows + 4) * chans, cols), bf),
            pltpu.VMEM(((rows + 2) * chans, cols), bf),
            pltpu.VMEM((chans, cols), bf),
            pltpu.VMEM((span, chans, cols), bf),
            pltpu.VMEM((span * chans, cols), bf),
            pltpu.VMEM((3 * chans, cols), bf),
            pltpu.VMEM((planes, chans, cols), bf),
            dma((2 * m,)), dma((2 * m,)), dma((2 * m,)), dma((2 * m + 2,)), dma((2,)), dma((2,)),
            dma((span,)), dma((span,)), dma((2,)), dma((2,)),
            dma((2 * m,)), dma((2 * m,)), dma((2 * m,)), dma((2 * m,)),
            pltpu.SemaphoreType.REGULAR((m, 2)),
        ],
        compiler_params=pltpu.CompilerParams(collective_id=0, has_side_effects=True),
    )(*operands)
    return updated.transpose(0, 2, 1)[None]


def fits(voxels):
    n = lax.axis_size("gx")
    sides = lax.axis_size("gy")
    xs, ys, zs, _ = voxels.shape
    return xs == 1 and sides == 2 and n % 2 == 0 and n >= 8 and ys == n * 4 * reach and 2 * ys == zs


def plain_planes(features, row_weights, column_weights, depth_weights, plane_kernels):
    xy_plane = jnp.einsum(
        "xyzc,zc->xyc", features, depth_weights, preferred_element_type=jnp.float32
    ).astype(jnp.bfloat16)
    xz_part = jnp.einsum(
        "xyzc,yc->xzc", features, column_weights, preferred_element_type=jnp.float32
    )
    yz_part = jnp.einsum("xyzc,xc->yzc", features, row_weights, preferred_element_type=jnp.float32)
    xy_out = plane_block(xy_plane, plane_kernels[0], rim_xy)
    xz_plane = lax.psum(xz_part, "gy").astype(jnp.bfloat16)
    xz_out = plane_block(xz_plane, plane_kernels[1], rim_xz)
    yz_plane = lax.psum(yz_part, "gx").astype(jnp.bfloat16)
    yz_out = plane_block(yz_plane, plane_kernels[2], rim_yz)
    return xy_out, xz_out, yz_out


def shards(
    voxels,
    occupancy,
    row_weights,
    column_weights,
    depth_weights,
    plane_kernels,
    expand_weight,
    shrink_weight,
):
    if fits(voxels):
        return fused(
            voxels,
            occupancy,
            row_weights,
            column_weights,
            depth_weights,
            plane_kernels,
            expand_weight,
            shrink_weight,
        )
    features = voxels * occupancy.astype(jnp.bfloat16)[..., None]
    xy_out, xz_out, yz_out = plain_planes(features, row_weights, column_weights, depth_weights, plane_kernels)
    product = xy_out.astype(jnp.float32)[:, :, None, :] * xz_out.astype(jnp.float32)[:, None, :, :]
    product = product * yz_out.astype(jnp.float32)[None, :, :, :]
    mixed = (product_scale * product).astype(jnp.bfloat16)
    hidden = jax.nn.silu(
        jnp.einsum("xyzc,ch->xyzh", mixed, expand_weight, preferred_element_type=jnp.float32)
    ).astype(jnp.bfloat16)
    branch = jnp.einsum("xyzh,hc->xyzc", hidden, shrink_weight, preferred_element_type=jnp.float32)
    return (features.astype(jnp.float32) + branch).astype(jnp.bfloat16)


def solution(mesh):
    in_specs = (
        P(("groups", "gx"), "gy", None, None),
        P(("groups", "gx"), "gy", None),
        P("gx", None),
        P("gy", None),
        P(),
        P(),
        P(),
        P(),
    )
    out_specs = P(("groups", "gx"), "gy", None, None)
    return jax.shard_map(shards, mesh=mesh, in_specs=in_specs, out_specs=out_specs, check_vma=False)
```

time: 46.6 us -> 38.6 us (0.83)
  Pallas kernels: 45.5 us -> 37.4 us
    pallas_call x1, Pallas kernels: 45.5 us -> 37.4 us  [fused(): pl.pallas_call(functools.partial(block_kernel, n), out_shape=pltpu.VMEM((...]
where the time goes in v1:
time: 38.6 us; the launch traced here: 38.4 us
  Pallas kernels  37.4 us (97%)
  local copies, waits for them, and re-layouts  0.97 us (3%)
    pallas_call x1, Pallas kernels, fused(): pl.pallas_call(functools.partial(block_kernel, n), out_shape=pltpu.VMEM((...  37.4 us
    unnamed x1, local copies, waits for them, and re-layouts  0.97 us

profile of v1, /device:TPU:0, one launch (start us, length us, event | category | flops | bytes accessed | tf_op | source)
XLA Modules:
  0.0 38.4 jit_solution(14853660415766244062)
XLA Ops:
  0.0 37.4 %shard_map.82 = bf16[64,64,128]{2,1,0:T(8,128)(2,1)S(1)} custom-call(bf16[64,64,128]{2,1,0:T(8,128)(2,1)} %bitcast.10, s32[64,128]{1,0:T(8,128)} %bitcast.11, bf16[1,64]{1,0:T(2,128)(2,1)} %row_weights_in.1, bf16[64,64]{1,0:T(8,128)(2,1)} %column_weights_in.1, bf16[64,128]{1,0:T(8,128)(2,1)} %bitcast.12, bf16[3,2,3,3,64,64]{5,4,3,2,1,0:T(8,128)(2,1)} %kernels_in.1, ...), custom_call_target="tpu_custom_call" | custom-call | tf_op jit(solution)/shard_map/pallas_call | solution.py:620
  37.4 1.0 %copy.10 = bf16[1,64,128,64]{2,3,1,0:T(8,128)(2,1)} copy(bf16[1,64,128,64]{2,3,1,0:T(8,128)(2,1)S(1)} %bitcast.9) | data formatting | bytes 2097152

commit v2 on v1

--- a/solution.py
+++ b/solution.py
@@ -108,23 +108,25 @@
 
 
 def joined(m, z, k):
-    return z in (0, m - 1) and abs(k - z) == 2
+    return z in (0, m - 1) and abs(k - z) > 1
 
 
 def joins(m, z):
-    found = []
-    for end, step in ((0, 1), (m - 1, -1)):
-        if z == end + step:
-            found.append((end, z + step))
-    return found
+    if z == 1:
+        return [(0, k) for k in range(m - 1, 1, -1)]
+    if z == m - 2:
+        return [(m - 1, k) for k in range(m - 2)]
+    return []
 
 
 def sum_order(m, z):
-    first = {k for _, k in joins(m, z)} | {k for k in others(m, z) if joined(m, z, k)}
-    ks = sorted(others(m, z), key=lambda k: (k not in first, -abs(k - z)))
-    rest = ks[1:]
-    chunks = [(ks[0], 0), (ks[0], 1)] + [(k, 0) for k in rest] + [(k, 1) for k in rest] + [(z, 0), (z, 1)]
-    return [2 * k + h for k, h in chunks]
+    far = sorted(others(m, z), key=lambda k: -abs(k - z))
+    held = [k for _, k in joins(m, z)]
+    first = [k for k in far if k in held or joined(m, z, k)]
+    rest = [k for k in far if k not in first]
+    ks = [(k, c) for c in range(3) for k in first] + [(k, c) for c in range(3) for k in rest + [z]]
+    ks = [kc for kc in ks if kc[0] != z] + [kc for kc in ks if kc[0] == z]
+    return [4 * k + c for k, c in ks]
 
 
 def passed(m, z, k):
@@ -147,9 +149,9 @@
     n, voxels_in, occupancy_in, row_weights_in, column_weights_in, depth_in, kernels_in, expand_in, shrink_in, updated,
     voxels, occupancy, row_weights, column_weights, depth_weights, plane_kernels, expand, shrink, load_s, fetch_s,
     part, rows_in, weights, wide, yz_out, row_sums, turned,
-    pair_in, pair_sum, line_in, yz_sum, yz_plane, yz_inner,
+    pair_in, pair_sum, line_in, slab_in, slab_sum, yz_sum, yz_plane, yz_inner,
     row_other, row_slots, row_plane, row_inner, outs,
-    pair_s, pair_r, line_s, line_r, halo_s, halo_r, row_s, row_r, core_s, core_r, spread_s, spread_r, cross_s, cross_r, known,
+    pair_s, pair_r, line_s, line_r, slab_s, slab_r, halo_s, halo_r, row_s, row_r, core_s, core_r, spread_s, spread_r, cross_s, cross_r, known,
 ):
     me = lax.axis_index("gx")
     g = lax.axis_index("gy")
@@ -185,6 +187,9 @@
 
     def chunk(bb, q):
         return pl.ds(piece(bb, q // 2) * rows + (q % 2) * sub, sub)
+
+    def slice_of(bb, q):
+        return pl.ds(piece(bb, q // 4) * rows + (q % 4) * reach, reach)
 
     def remote(src, dst, send, recv, gx, gy=None):
         target = {"gx": gx} if gy is None else {"gx": gx, "gy": gy}
@@ -220,20 +225,17 @@
     )
 
     order = table(lambda z: sum_order(m, z))
-    turns = [pick(a, [o[i] for o in order]) for i in range(2 * m)]
-    lanes = [pick(a, [sum_order(m, z)[i] // 2 for z in range(m)]) for i in (0, 2)]
-    lanes += [pick(a, [sum_order(m, z)[2 + i] // 2 for z in range(m)]) for i in range(1, m - 2)]
-    lanes = lanes + [a]
+    steps = 3 * m
+    turns = [pick(a, [o[i] for o in order]) for i in range(steps)]
 
     small = [
         pltpu.make_async_copy(row_weights_in, row_weights, load_s.at[0]),
         pltpu.make_async_copy(occupancy_in, occupancy, load_s.at[1]),
     ]
     large = []
-    for bb in (1 - b, b):
-        for k in lanes:
-            at = pl.ds(piece(bb, k) * rows, rows)
-            large.append(pltpu.make_async_copy(voxels_in.at[at], voxels.at[at], load_s.at[2 + len(large)]))
+    for j in range(n):
+        at = pl.ds(j * rows, rows)
+        large.append(pltpu.make_async_copy(voxels_in.at[at], voxels.at[at], load_s.at[2 + j]))
     fetches = [
         pltpu.make_async_copy(kernels_in, plane_kernels, fetch_s.at[0]),
         pltpu.make_async_copy(column_weights_in, column_weights, fetch_s.at[1]),
@@ -256,23 +258,37 @@
 
     pair_copies = []
     for q in turns:
-        pair_copies.append(remote(part.at[chunk(1 - b, q)], pair_in.at[q], pair_s.at[q], pair_r.at[q], partner))
-
-    large[0].wait()
-    yz_terms(piece(1 - b, lanes[0]))
+        pair_copies.append(remote(part.at[slice_of(1 - b, q)], pair_in.at[q], pair_s.at[q], pair_r.at[q], partner))
+
+    def yz_pieces(j, carry):
+        yz_terms(j)
+        return carry
+
+    for copy in large:
+        copy.wait()
+    lax.fori_loop(0, n, yz_pieces, 0)
+
+    slab_copies = []
+    for dist in range(1, m):
+        for side in (-1, 1):
+            k = jnp.clip(a + side * dist, 0, m - 1)
+            there = (a + side * dist >= 0) & (a + side * dist < m)
+            for bb in range(2):
+                at = 2 * (dist + (m - 1 if side > 0 else 0) - 1) + bb
+                copy = remote(
+                    part.at[slice_of(bb, 4 * k + 3)], slab_in.at[2 * a + bb], slab_s.at[at], slab_r.at[2 * a + bb], k * 2 + b
+                )
+                slab_copies.append((dist, there, copy))
+
+    def start_slabs(dist):
+        for d, there, copy in slab_copies:
+            if d == dist:
+                pl.when(there)(copy.start)
+
     pl.semaphore_wait(barrier, greeters)
-    pair_copies[0].start()
-    pair_copies[1].start()
-    for i in range(1, m - 1):
-        large[i].wait()
-        yz_terms(piece(1 - b, lanes[i]))
-        pair_copies[1 + i].start()
-    for i in range(1, m - 1):
-        pair_copies[m - 1 + i].start()
-    large[m - 1].wait()
-    yz_terms(piece(1 - b, lanes[m - 1]))
-    pair_copies[2 * m - 2].start()
-    pair_copies[2 * m - 1].start()
+    for copy in pair_copies:
+        copy.start()
+    start_slabs(1)
 
     def tell(level, side):
         step = 2 if side == 0 else -2
@@ -294,10 +310,6 @@
                 pl.when(tells(level, side))(lambda: tell(level, side))
 
     tell_level(2)
-
-    for i in range(m):
-        large[m + i].wait()
-        yz_terms(piece(b, lanes[i]))
 
     for copy in fetches:
         copy.wait()
@@ -329,80 +341,125 @@
             taps = plane_kernels[p, layer, :, off].reshape(3 * chans, chans)
             weights[p, layer, off * chans : (off + 1) * chans, :] = flipped(taps).astype(bf)
 
-    for level in range(3, m):
-        tell_level(level)
-
     holds = table(lambda z: [k for _, k in joins(m, z)])
-    held = pick(a, [ks[0] if ks else -1 for ks in holds])
-    source = pick(a, [joins(m, z)[0][0] if joins(m, z) else -1 for z in range(m)])
-
-    def line_target(i):
-        k = turns[i] // 2
-        gx = pick(a, [((z + (1 if order[z][i] // 2 > z else -1)) if joined(m, z, order[z][i] // 2) else order[z][i] // 2) for z in range(m)])
-        slot = pick(a, [2 * (m if joined(m, z, order[z][i] // 2) else z) + order[z][i] % 2 for z in range(m)])
-        return k, gx * 2 + b, slot
-
-    line_copies = []
-    for i in range(2 * m - 2):
-        k, gx, slot = line_target(i)
+    holding = (a == 1) | (a == m - 2)
+
+    def line_copy(i):
+        gx, slot = [], []
+        for z in range(m):
+            k, c = order[z][i] // 4, order[z][i] % 4
+            if k == z:
+                gx.append(z)
+                slot.append(0)
+            elif joined(m, z, k):
+                via = z + (1 if k > z else -1)
+                gx.append(via)
+                slot.append(4 * m + 4 * holds[via].index(k) + c)
+            else:
+                gx.append(k)
+                slot.append(4 * z + c)
+        to = pick(a, slot)
         q = turns[i]
-        line_copies.append(remote(pair_sum.at[q], line_in.at[slot], line_s.at[q], line_r.at[slot], gx))
+        return remote(pair_sum.at[q], line_in.at[to], line_s.at[q], line_r.at[to], pick(a, gx) * 2 + b)
+
+    line_copies = [line_copy(i) for i in range(steps - 3)]
+    held = [pick(a, [int(order[z][i] // 4 in holds[z]) for z in range(m)]) for i in range(steps - 3)]
 
     def reduce_pair(i):
         q = turns[i]
         pair_copies[i].wait_recv()
-        mine = part[chunk(b, q)].astype(f32)
+        mine = part[slice_of(b, q)].astype(f32)
         pair_sum[q] = (mine + pair_in[q].astype(f32)).astype(bf)
-        pl.when(q // 2 != held)(line_copies[i].start)
-
-    def reduce_joined(h):
-        @pl.when(held >= 0)
+        pl.when(held[i] == 0)(line_copies[i].start)
+
+    def reduce_joined(i):
+        @pl.when(holding)
         def _():
-            q = 2 * jnp.maximum(held, 0) + h
-            slot = 2 * m + h
+            q = turns[i]
+            slot = 4 * m + pick(a, [4 * (holds[z].index(order[z][i] // 4) if holds[z] else 0) + order[z][i] % 4 for z in range(m)])
             remote(pair_sum.at[q], line_in.at[slot], line_s.at[q], line_r.at[slot], partner).wait_recv()
             pair_sum[q] = (pair_sum[q].astype(f32) + line_in[slot].astype(f32)).astype(bf)
-            line_copies[h].start()
-
-    def reduce_own(h):
-        q = turns[2 * m - 2 + h]
-        pair_copies[2 * m - 2 + h].wait_recv()
-        yz_sum[h] = part[chunk(b, q)].astype(f32) + pair_in[q].astype(f32)
-
-    def reduce_line(h):
+            line_copies[i].start()
+
+    def reduce_own(c):
+        pair_copies[steps - 3 + c].wait_recv()
+        q = 4 * a + c
+        yz_sum[c] = part[slice_of(b, q)].astype(f32) + pair_in[q].astype(f32)
+
+    def reduce_line(c):
         for i in range(m - 1):
-            src = pick(a, [sorted(others(m, z), key=lambda s: (abs(s - z), s))[i] for z in range(m)])
-            skip = pick(a, [int(joined(m, sorted(others(m, z), key=lambda s: (abs(s - z), s))[i], z)) for z in range(m)])
+            sources = [sorted(others(m, z), key=lambda s: (abs(s - z), s))[i] for z in range(m)]
+            src = pick(a, sources)
+            skip = pick(a, [int(joined(m, s, z)) for z, s in enumerate(sources)])
 
             @pl.when(skip == 0)
             def _():
-                slot = 2 * src + h
+                slot = 4 * src + c
                 remote(pair_sum.at[slot], line_in.at[slot], line_s.at[slot], line_r.at[slot], partner).wait_recv()
-                yz_sum[h] = yz_sum[h] + line_in[slot].astype(f32)
-
-    row_terms(0)
-    reduce_pair(0)
-    row_terms(share)
-    reduce_pair(1)
-    tell_level(m)
-    row_terms(2 * share)
-    reduce_pair(2)
-    wide[...] = flipped(expand[...]).astype(bf)
-    flip_plane(2, 0)
-    reduce_joined(0)
-    for i in range(3, 2 * m - 2):
+                yz_sum[c] = yz_sum[c] + line_in[slot].astype(f32)
+
+    slab_cross = remote(slab_sum, pair_in.at[4 * a + 3], pair_s.at[4 * a + 3], pair_r.at[4 * a + 3], partner)
+
+    def reduce_slab():
+        q = 4 * a + 3
+        total = [part[slice_of(bb, q)].astype(f32) for bb in (1 - b, b)]
+        for i in range(m - 1):
+            src = pick(a, [others(m, z)[i] for z in range(m)])
+            for side, bb in enumerate((1 - b, b)):
+                slot = 2 * src + bb
+                remote(slab_in.at[slot], slab_in.at[slot], slab_s.at[slot], slab_r.at[slot], partner).wait_recv()
+                total[side] = total[side] + slab_in[slot].astype(f32)
+        slab_sum[...] = total[0].astype(bf)
+        slab_cross.start()
+        yz_sum[3] = total[1]
+
+    def reduce_slab_own():
+        slab_cross.wait_recv()
+        yz_sum[3] = yz_sum[3] + pair_in[4 * a + 3].astype(f32)
+
+    for i in range(m):
         row_terms(i * share)
-        reduce_pair(i)
-        if i == 3:
-            flip_plane(2, 1)
-            reduce_joined(1)
-    for i in range(2 * m - 2, 2 * m):
+    for level in range(3, m + 1):
+        tell_level(level)
+        start_slabs(level - 1)
+    for i in range(m, 2 * m):
         row_terms(i * share)
     rows_in[...] = row_sums[...].astype(bf)
     core = remote(rows_in.at[1 - g], row_other.at[...], core_s.at[0], core_r.at[0], me, 1 - g)
     core.start()
+    flip_plane(2, 0)
+    flip_plane(2, 1)
+
+    first = 5
+    for i in range(first):
+        reduce_pair(i)
+    merges = 3 * (m - 2)
+    slab_at = steps - 3 - 1
+    done = 0
+    for i in range(first, steps - 3):
+        if done < merges:
+            reduce_joined(done)
+            done += 1
+        reduce_pair(i)
+    reduce_slab()
+    core.wait_recv()
+    mid = rows_in[g].astype(f32) + row_other[...].astype(f32)
+    row_slots[reach] = mid.astype(bf)
+    row_copies = []
+    for dx in range(-reach, reach + 1):
+        if dx != 0:
+            slot = reach - dx
+            copy = remote(
+                row_slots.at[reach], row_slots.at[slot], row_s.at[slot], row_r.at[slot], jnp.clip(me + dx, 0, n - 1)
+            )
+            row_copies.append((dx, copy))
+            pl.when((me + dx >= 0) & (me + dx < n))(copy.start)
+    while done < merges:
+        reduce_joined(done)
+        done += 1
     for layer in range(2):
         flip_plane(g, layer)
+    wide[...] = flipped(expand[...]).astype(bf)
 
     edge = reach * chans
     halo = [
@@ -424,32 +481,24 @@
     def _():
         yz_plane[pl.ds(edge + rows * chans, edge), :] = jnp.zeros((edge, cols), bf)
 
-    def settle(h):
-        for r in range(sub):
+    def settle(c):
+        for i in range(reach):
+            h, r = c // 2, (c % 2) * reach + i
             at = (reach + offset(h, r)) * chans
-            yz_plane[at : at + chans, :] = yz_sum[h, r].astype(bf)
-
-    reduce_own(0)
-    core.wait_recv()
-    mid = rows_in[g].astype(f32) + row_other[...].astype(f32)
-    row_slots[reach] = mid.astype(bf)
-    row_copies = []
-    for dx in range(-reach, reach + 1):
-        if dx != 0:
-            slot = reach - dx
-            copy = remote(
-                row_slots.at[reach], row_slots.at[slot], row_s.at[slot], row_r.at[slot], jnp.clip(me + dx, 0, n - 1)
-            )
-            row_copies.append((dx, copy))
-    reduce_line(0)
-    settle(0)
+            yz_plane[at : at + chans, :] = yz_sum[c, i].astype(bf)
+
+    for c in range(2):
+        reduce_own(c)
+    for c in range(2):
+        reduce_line(c)
+        settle(c)
     for sends, _, copy in halo:
         pl.when(sends)(copy.start)
-    for dx, copy in row_copies:
-        pl.when((me + dx >= 0) & (me + dx < n))(copy.start)
-    reduce_own(1)
-    reduce_line(1)
-    settle(1)
+    reduce_own(2)
+    reduce_line(2)
+    settle(2)
+    reduce_slab_own()
+    settle(3)
 
     def inner_row(i, keep):
         inner = silu(conv_row(yz_plane[i * chans : (i + 3) * chans, :], weights[2, 0])) * keep
@@ -579,8 +628,11 @@
 
     for copy in pair_copies:
         copy.wait_send()
+    slab_cross.wait_send()
     for copy in line_copies:
         copy.wait_send()
+    for _, there, copy in slab_copies:
+        pl.when(there)(copy.wait_send)
     for sends, _, copy in halo:
         pl.when(sends)(copy.wait_send)
     core.wait_send()
@@ -624,7 +676,7 @@
         out_specs=pl.BlockSpec(memory_space=pltpu.VMEM),
         scratch_shapes=[pltpu.VMEM(x.shape, x.dtype) for x in operands]
         + [
-            dma((2 + 2 * m,)),
+            dma((2 + n,)),
             dma((5,)),
             pltpu.VMEM((count, chans, cols), bf),
             pltpu.VMEM((planes, chans, cols), bf),
@@ -633,10 +685,12 @@
             pltpu.VMEM((count, chans, cols), bf),
             pltpu.VMEM((planes, chans, cols), f32),
             pltpu.VMEM((chans, count), f32),
-            pltpu.VMEM((2 * m, sub, chans, cols), bf),
-            pltpu.VMEM((2 * m, sub, chans, cols), bf),
-            pltpu.VMEM((2 * m + 2, sub, chans, cols), bf),
-            pltpu.VMEM((2, sub, chans, cols), f32),
+            pltpu.VMEM((4 * m, reach, chans, cols), bf),
+            pltpu.VMEM((4 * m, reach, chans, cols), bf),
+            pltpu.VMEM((8 * m, reach, chans, cols), bf),
+            pltpu.VMEM((2 * m, reach, chans, cols), bf),
+            pltpu.VMEM((reach, chans, cols), bf),
+            pltpu.VMEM((4, reach, chans, cols), f32),
             pltpu.VMEM(((rows + 4) * chans, cols), bf),
             pltpu.VMEM(((rows + 2) * chans, cols), bf),
             pltpu.VMEM((chans, cols), bf),
@@ -644,7 +698,7 @@
             pltpu.VMEM((span * chans, cols), bf),
             pltpu.VMEM((3 * chans, cols), bf),
             pltpu.VMEM((planes, chans, cols), bf),
-            dma((2 * m,)), dma((2 * m,)), dma((2 * m,)), dma((2 * m + 2,)), dma((2,)), dma((2,)),
+            dma((4 * m,)), dma((4 * m,)), dma((4 * m,)), dma((8 * m,)), dma((4 * m,)), dma((2 * m,)), dma((2,)), dma((2,)),
             dma((span,)), dma((span,)), dma((2,)), dma((2,)),
             dma((2 * m,)), dma((2 * m,)), dma((2 * m,)), dma((2 * m,)),
             pltpu.SemaphoreType.REGULAR((m, 2)),

time: 38.6 us -> 38.5 us (level)
  no operation moved by 1% of the time
where the time goes in v2:
time: 38.5 us; the launch traced here: 38.4 us
  Pallas kernels  37.4 us (97%)
  local copies, waits for them, and re-layouts  0.97 us (3%)
    pallas_call x1, Pallas kernels, fused(): pl.pallas_call(functools.partial(block_kernel, n), out_shape=pltpu.VMEM((...  37.4 us
    unnamed x1, local copies, waits for them, and re-layouts  0.97 us

profile of v2, /device:TPU:0, one launch (start us, length us, event | category | flops | bytes accessed | tf_op | source)
XLA Modules:
  0.0 38.4 jit_solution(8951160495417162717)
XLA Ops:
  0.0 37.4 %shard_map.82 = bf16[64,64,128]{2,1,0:T(8,128)(2,1)S(1)} custom-call(bf16[64,64,128]{2,1,0:T(8,128)(2,1)} %bitcast.10, s32[64,128]{1,0:T(8,128)} %bitcast.11, bf16[1,64]{1,0:T(2,128)(2,1)} %row_weights_in.1, bf16[64,64]{1,0:T(8,128)(2,1)} %column_weights_in.1, bf16[64,128]{1,0:T(8,128)(2,1)} %bitcast.12, bf16[3,2,3,3,64,64]{5,4,3,2,1,0:T(8,128)(2,1)} %kernels_in.1, ...), custom_call_target="tpu_custom_call" | custom-call | tf_op jit(solution)/shard_map/pallas_call | solution.py:672
  37.4 1.0 %copy.10 = bf16[1,64,128,64]{2,3,1,0:T(8,128)(2,1)} copy(bf16[1,64,128,64]{2,3,1,0:T(8,128)(2,1)S(1)} %bitcast.9) | data formatting | bytes 2097152

commit v3 on v2

--- a/solution.py
+++ b/solution.py
@@ -95,6 +95,9 @@
     return jnp.sum(jnp.where(lane == at, x, 0.0), axis=1, keepdims=True)
 
 
+own_order = (2, 3, 1, 0)
+
+
 def pick(index, values):
     chosen = values[0]
     for i, value in enumerate(values):
@@ -130,19 +133,16 @@
 
 
 def passed(m, z, k):
-    return k in (0, m - 1) and abs(k - z) == 2
+    return k == m - 1 and z == m - 3
 
 
 def give_order(m, z):
-    return sorted(others(m, z), key=lambda k: -abs(k - z))
+    return sorted(others(m, z), key=lambda k: k - z if k > z else k)
 
 
 def take_order(m, z):
-    direct = sorted([k for k in others(m, z) if not passed(m, k, z)], key=lambda k: (k in (0, m - 1), -abs(k - z)))
-    late = [k for k in others(m, z) if passed(m, k, z)]
-    ks = direct + late
-    chunks = [(k, h) for k in ks[:2] for h in (1,)] + [(k, 0) for k in ks[:2]] + [(k, h) for k in ks[2:] for h in (1, 0)]
-    return [2 * k + h for k, h in chunks]
+    ks = sorted(others(m, z), key=lambda k: (passed(m, k, z), abs(k - z)))
+    return [4 * k + c for c in own_order for k in ks]
 
 
 def block_kernel(
@@ -160,7 +160,6 @@
     b = me % 2
     count, chans, cols = part.shape
     rows = count // n
-    sub = 2 * reach
     bf = jnp.bfloat16
     f32 = jnp.float32
     partner = a * 2 + 1 - b
@@ -179,14 +178,9 @@
         aa = j % m
         return (aa + bb * (m - 1 - 2 * aa)) * 2 + bb
 
-    def offset(h, r):
-        edge = r if r < reach else rows - sub + r
-        if isinstance(h, int):
-            return edge if h == 0 else reach + r
-        return jnp.where(h == 0, edge, reach + r)
-
-    def chunk(bb, q):
-        return pl.ds(piece(bb, q // 2) * rows + (q % 2) * sub, sub)
+    def offset(c):
+        starts = [0, rows - reach, reach, 2 * reach]
+        return starts[c] if isinstance(c, int) else pick(c, starts)
 
     def slice_of(bb, q):
         return pl.ds(piece(bb, q // 4) * rows + (q % 4) * reach, reach)
@@ -233,9 +227,10 @@
         pltpu.make_async_copy(occupancy_in, occupancy, load_s.at[1]),
     ]
     large = []
-    for j in range(n):
-        at = pl.ds(j * rows, rows)
-        large.append(pltpu.make_async_copy(voxels_in.at[at], voxels.at[at], load_s.at[2 + j]))
+    for bb in (1 - b, b):
+        for k in range(m):
+            at = pl.ds(piece(bb, k) * rows, rows)
+            large.append(pltpu.make_async_copy(voxels_in.at[at], voxels.at[at], load_s.at[2 + len(large)]))
     fetches = [
         pltpu.make_async_copy(kernels_in, plane_kernels, fetch_s.at[0]),
         pltpu.make_async_copy(column_weights_in, column_weights, fetch_s.at[1]),
@@ -252,21 +247,24 @@
     rw = jnp.sum(rw * identity(chans), axis=1, keepdims=True)
 
     def yz_terms(j):
-        for h in range(2):
-            for r in range(sub):
-                part[j * rows + h * sub + r] = (feature_row(j * rows + offset(h, r)) * rw).astype(bf)
+        for c in range(4):
+            for r in range(reach):
+                part[j * rows + c * reach + r] = (feature_row(j * rows + offset(c) + r) * rw).astype(bf)
 
     pair_copies = []
     for q in turns:
         pair_copies.append(remote(part.at[slice_of(1 - b, q)], pair_in.at[q], pair_s.at[q], pair_r.at[q], partner))
 
-    def yz_pieces(j, carry):
-        yz_terms(j)
-        return carry
-
-    for copy in large:
+    def yz_pieces(bb):
+        def some(k, carry):
+            yz_terms(piece(bb, k))
+            return carry
+
+        lax.fori_loop(0, m, some, 0)
+
+    for copy in large[:m]:
         copy.wait()
-    lax.fori_loop(0, n, yz_pieces, 0)
+    yz_pieces(1 - b)
 
     slab_copies = []
     for dist in range(1, m):
@@ -288,6 +286,9 @@
     pl.semaphore_wait(barrier, greeters)
     for copy in pair_copies:
         copy.start()
+    for copy in large[m:]:
+        copy.wait()
+    yz_pieces(b)
     start_slabs(1)
 
     def tell(level, side):
@@ -482,62 +483,61 @@
         yz_plane[pl.ds(edge + rows * chans, edge), :] = jnp.zeros((edge, cols), bf)
 
     def settle(c):
-        for i in range(reach):
-            h, r = c // 2, (c % 2) * reach + i
-            at = (reach + offset(h, r)) * chans
-            yz_plane[at : at + chans, :] = yz_sum[c, i].astype(bf)
+        for r in range(reach):
+            at = (reach + offset(c) + r) * chans
+            yz_plane[at : at + chans, :] = yz_sum[c, r].astype(bf)
+
+    def inner_row(i, keep):
+        inner = silu(conv_row(yz_plane[i * chans : (i + 3) * chans, :], weights[2, 0])) * keep
+        yz_inner[i * chans : (i + 1) * chans, :] = inner.astype(bf)
 
     for c in range(2):
         reduce_own(c)
     for c in range(2):
         reduce_line(c)
         settle(c)
-    for sends, _, copy in halo:
-        pl.when(sends)(copy.start)
+        pl.when(halo[c][0])(halo[c][2].start)
     reduce_own(2)
+    reduce_slab_own()
+    settle(3)
+    for i in range(rows - reach, rows):
+        inner_row(i, 1.0)
     reduce_line(2)
     settle(2)
-    reduce_slab_own()
-    settle(3)
-
-    def inner_row(i, keep):
-        inner = silu(conv_row(yz_plane[i * chans : (i + 3) * chans, :], weights[2, 0])) * keep
-        yz_inner[i * chans : (i + 1) * chans, :] = inner.astype(bf)
 
     spread_copies = []
     own = piece(b, a)
 
-    def give_chunk(h):
-        for r in range(sub):
-            at = offset(h, r) * chans
+    def cross_copy(bb, q):
+        at = slice_of(bb, q)
+        return remote(yz_out.at[at], yz_out.at[at], cross_s.at[q], cross_r.at[q], partner)
+
+    def give_chunk(c):
+        for r in range(reach):
+            at = (offset(c) + r) * chans
             done = conv_row(yz_inner[at : at + 3 * chans, :], weights[2, 1])
-            yz_out[own * rows + h * sub + r] = done.astype(bf)
-        q = 2 * a + h
+            yz_out[own * rows + c * reach + r] = done.astype(bf)
+        q = 4 * a + c
         cross_copy(b, q).start()
         for i in range(m - 1):
             k = pick(a, [give_order(m, z)[i] for z in range(m)])
             skip = pick(a, [int(passed(m, z, give_order(m, z)[i])) for z in range(m)])
-            at = chunk(b, q)
-            copy = remote(yz_out.at[at], yz_out.at[at], spread_s.at[2 * i + h], spread_r.at[q], k * 2 + b)
+            at = slice_of(b, q)
+            copy = remote(yz_out.at[at], yz_out.at[at], spread_s.at[4 * i + c], spread_r.at[q], k * 2 + b)
             pl.when(skip == 0)(copy.start)
             spread_copies.append((skip == 0, copy))
 
-    def cross_copy(bb, q):
-        at = chunk(bb, q)
-        return remote(yz_out.at[at], yz_out.at[at], cross_s.at[q], cross_r.at[q], partner)
-
-    for i in range(reach, rows):
+    for i in range(reach, rows - reach):
         inner_row(i, 1.0)
+    give_chunk(2)
+    give_chunk(3)
+    pl.when(halo[0][1])(halo[0][2].wait_recv)
+    inner_row(rows, 1.0)
+    inner_row(rows + 1, (place < last).astype(f32))
     give_chunk(1)
-    for _, receives, copy in halo:
-        pl.when(receives)(copy.wait_recv)
-    for i in list(range(reach)) + list(range(rows, rows + 2)):
-        keep = 1.0
-        if i == 0:
-            keep = (place > 0).astype(f32)
-        if i == rows + 1:
-            keep = (place < last).astype(f32)
-        inner_row(i, keep)
+    pl.when(halo[1][1])(halo[1][2].wait_recv)
+    inner_row(0, (place > 0).astype(f32))
+    inner_row(1, 1.0)
     give_chunk(0)
 
     for dx, copy in row_copies:
@@ -566,65 +566,51 @@
     remote(outs.at[1 - g], outs.at[1 - g], core_s.at[1], core_r.at[1], me, 1 - g).wait_recv()
 
     def finish(bb, q):
-        j = piece(bb, q // 2)
-        h = q % 2
+        c = q % 4
+        stored = piece(bb, q // 4) * rows + c * reach
+        first = piece(bb, q // 4) * rows + offset(c)
         xy_out = outs[0].astype(f32)
         xz_out = outs[1].astype(f32)
-        at = [(j * rows + h * sub + r, j * rows + offset(h, r)) for r in range(sub)]
         mixed = []
-        for s, y in at:
-            product = column(xy_out, g * count + y) * xz_out
-            product = product * yz_out[s].astype(f32)
+        for r in range(reach):
+            product = column(xy_out, g * count + first + r) * xz_out
+            product = product * yz_out[stored + r].astype(f32)
             mixed.append((product_scale * product).astype(bf))
         mixed = jnp.concatenate(mixed, axis=1)
         hidden = silu(jnp.dot(wide[...], mixed, preferred_element_type=f32)).astype(bf)
         branch = jnp.dot(shrink[...], hidden, preferred_element_type=f32)
-        for k, (s, y) in enumerate(at):
-            updated[y] = (feature_row(y) + branch[:, k * cols : (k + 1) * cols]).astype(bf)
-
-    takes = [pick(a, [take_order(m, z)[i] for z in range(m)]) for i in range(2 * m - 2)]
-    hands = table(lambda z: [k for k in others(m, z) if any(passed(m, k, t) and abs(z - t) == 1 for t in others(m, z))])
-    handed = pick(a, [ks[0] if ks else -1 for ks in hands])
-    onward = pick(a, [(0 if z == 1 else m - 1) if hands[z] else 0 for z in range(m)])
-
-    def hand_copy(h):
-        q = 2 * jnp.maximum(handed, 0) + h
-        at = chunk(b, q)
-        return remote(yz_out.at[at], yz_out.at[at], spread_s.at[2 * (m - 1) + h], spread_r.at[q], onward * 2 + b)
+        for r in range(reach):
+            updated[first + r] = (feature_row(first + r) + branch[:, r * cols : (r + 1) * cols]).astype(bf)
+
+    takes = [pick(a, [take_order(m, z)[i] for z in range(m)]) for i in range(4 * m - 4)]
+    hands = a == m - 2
+    handed = max(m - 3, 0)
+
+    def hand_copy(q):
+        at = slice_of(b, q)
+        return remote(yz_out.at[at], yz_out.at[at], spread_s.at[4 * (m - 1) + q % 4], spread_r.at[q], (m - 1) * 2 + b)
 
     def take(i):
         q = takes[i]
-        at = chunk(b, q)
+        at = slice_of(b, q)
         remote(yz_out.at[at], yz_out.at[at], spread_s.at[0], spread_r.at[q], partner).wait_recv()
         cross_copy(b, q).start()
-        for h in range(2):
-            pl.when((handed >= 0) & (q == 2 * handed + h))(hand_copy(h).start)
+        pl.when(hands & (q // 4 == handed))(hand_copy(q).start)
         finish(b, q)
 
-    crossed = [2 * a + 1, 2 * a] + takes
+    crossed = [4 * a + c for c in own_order] + takes
 
     def take_crossed(i):
         q = crossed[i]
         cross_copy(1 - b, q).wait_recv()
         finish(1 - b, q)
 
-    finish(b, 2 * a + 1)
-    finish(b, 2 * a)
-    takes_done = 0
-    crossed_done = 0
-    for step in "tctcttctct" + "c" * 4:
-        if step == "t":
-            take(takes_done)
-            takes_done += 1
-        else:
-            take_crossed(crossed_done)
-            crossed_done += 1
-    while takes_done < len(takes):
-        take(takes_done)
-        takes_done += 1
-    while crossed_done < len(crossed):
-        take_crossed(crossed_done)
-        crossed_done += 1
+    for c in own_order:
+        finish(b, 4 * a + c)
+    for i in range(len(crossed)):
+        if i < len(takes):
+            take(i)
+        take_crossed(i)
 
     for copy in pair_copies:
         copy.wait_send()
@@ -641,8 +627,8 @@
         pl.when((me + dx >= 0) & (me + dx < n))(copy.wait_send)
     for sent, copy in spread_copies:
         pl.when(sent)(copy.wait_send)
-    for h in range(2):
-        pl.when(handed >= 0)(hand_copy(h).wait_send)
+    for c in range(4):
+        pl.when(hands)(hand_copy(4 * handed + c).wait_send)
     for q in crossed:
         cross_copy(b, q).wait_send()
 
@@ -652,7 +638,6 @@
     m = n // 2
     count, cols, chans = voxels.shape[1:]
     rows = count // n
-    sub = 2 * reach
     sets, layers = plane_kernels.shape[:2]
     planes = 2
     span = 2 * reach + 1
@@ -700,7 +685,7 @@
             pltpu.VMEM((planes, chans, cols), bf),
             dma((4 * m,)), dma((4 * m,)), dma((4 * m,)), dma((8 * m,)), dma((4 * m,)), dma((2 * m,)), dma((2,)), dma((2,)),
             dma((span,)), dma((span,)), dma((2,)), dma((2,)),
-            dma((2 * m,)), dma((2 * m,)), dma((2 * m,)), dma((2 * m,)),
+            dma((4 * m,)), dma((4 * m,)), dma((4 * m,)), dma((4 * m,)),
             pltpu.SemaphoreType.REGULAR((m, 2)),
         ],
         compiler_params=pltpu.CompilerParams(collective_id=0, has_side_effects=True),

time: 38.5 us -> 40.4 us (1.049)
  Pallas kernels: 37.4 us -> 39.3 us
    pallas_call x1, Pallas kernels: 37.4 us -> 39.3 us  [fused(): pl.pallas_call(functools.partial(block_kernel, n), out_shape=pltpu.VMEM((...]
where the time goes in v3:
time: 40.4 us; the launch traced here: 40.3 us
  Pallas kernels  39.3 us (97%)
  local copies, waits for them, and re-layouts  0.97 us (2%)
    pallas_call x1, Pallas kernels, fused(): pl.pallas_call(functools.partial(block_kernel, n), out_shape=pltpu.VMEM((...  39.3 us
    unnamed x1, local copies, waits for them, and re-layouts  0.97 us

profile of v3, /device:TPU:0, one launch (start us, length us, event | category | flops | bytes accessed | tf_op | source)
XLA Modules:
  0.0 40.3 jit_solution(9906482830616862035)
XLA Ops:
  0.0 39.3 %shard_map.82 = bf16[64,64,128]{2,1,0:T(8,128)(2,1)S(1)} custom-call(bf16[64,64,128]{2,1,0:T(8,128)(2,1)} %bitcast.10, s32[64,128]{1,0:T(8,128)} %bitcast.11, bf16[1,64]{1,0:T(2,128)(2,1)} %row_weights_in.1, bf16[64,64]{1,0:T(8,128)(2,1)} %column_weights_in.1, bf16[64,128]{1,0:T(8,128)(2,1)} %bitcast.12, bf16[3,2,3,3,64,64]{5,4,3,2,1,0:T(8,128)(2,1)} %kernels_in.1, ...), custom_call_target="tpu_custom_call" | custom-call | tf_op jit(solution)/shard_map/pallas_call | solution.py:657
  39.3 1.0 %copy.10 = bf16[1,64,128,64]{2,3,1,0:T(8,128)(2,1)} copy(bf16[1,64,128,64]{2,3,1,0:T(8,128)(2,1)S(1)} %bitcast.9) | data formatting | bytes 2097152

commit v4 on v3

--- a/solution.py
+++ b/solution.py
@@ -95,7 +95,8 @@
     return jnp.sum(jnp.where(lane == at, x, 0.0), axis=1, keepdims=True)
 
 
-own_order = (2, 3, 1, 0)
+halves = ((2, 3), (1, 0))
+own_order = halves[0] + halves[1]
 
 
 def pick(index, values):
@@ -141,8 +142,11 @@
 
 
 def take_order(m, z):
-    ks = sorted(others(m, z), key=lambda k: (passed(m, k, z), abs(k - z)))
-    return [4 * k + c for c in own_order for k in ks]
+    def rank(k):
+        return passed(m, k, z), z if k > z else z - k - 1, abs(k - z) > 1, -k
+
+    ks = sorted(others(m, z), key=rank)
+    return [4 * k + c for half in halves for k in ks for c in half]
 
 
 def block_kernel(
@@ -253,7 +257,7 @@
 
     pair_copies = []
     for q in turns:
-        pair_copies.append(remote(part.at[slice_of(1 - b, q)], pair_in.at[q], pair_s.at[q], pair_r.at[q], partner))
+        pair_copies.append(remote(part.at[slice_of(1 - b, q)], pair_in.at[q], pair_s.at[0], pair_r.at[q], partner))
 
     def yz_pieces(bb):
         def some(k, carry):
@@ -266,15 +270,21 @@
         copy.wait()
     yz_pieces(1 - b)
 
+    def sent(buffer, size, sem, recv):
+        return remote(buffer.at[pl.ds(0, size)], buffer.at[pl.ds(0, size)], sem.at[0], recv.at[0], partner)
+
+    pair_all = sent(part, steps * reach, pair_s, pair_r)
+    line_all = sent(pair_sum, steps - 3, line_s, line_r)
+    slab_all = sent(part, 2 * (m - 1) * reach, slab_s, slab_r)
+    cross_all = sent(yz_out, 4 * m * reach, cross_s, cross_r)
     slab_copies = []
     for dist in range(1, m):
         for side in (-1, 1):
             k = jnp.clip(a + side * dist, 0, m - 1)
             there = (a + side * dist >= 0) & (a + side * dist < m)
             for bb in range(2):
-                at = 2 * (dist + (m - 1 if side > 0 else 0) - 1) + bb
                 copy = remote(
-                    part.at[slice_of(bb, 4 * k + 3)], slab_in.at[2 * a + bb], slab_s.at[at], slab_r.at[2 * a + bb], k * 2 + b
+                    part.at[slice_of(bb, 4 * k + 3)], slab_in.at[2 * a + bb], slab_s.at[0], slab_r.at[2 * a + bb], k * 2 + b
                 )
                 slab_copies.append((dist, there, copy))
 
@@ -311,6 +321,9 @@
                 pl.when(tells(level, side))(lambda: tell(level, side))
 
     tell_level(2)
+    for level in range(3, m):
+        tell_level(level)
+        start_slabs(level - 1)
 
     for copy in fetches:
         copy.wait()
@@ -361,7 +374,7 @@
                 slot.append(4 * z + c)
         to = pick(a, slot)
         q = turns[i]
-        return remote(pair_sum.at[q], line_in.at[to], line_s.at[q], line_r.at[to], pick(a, gx) * 2 + b)
+        return remote(pair_sum.at[q], line_in.at[to], line_s.at[0], line_r.at[to], pick(a, gx) * 2 + b)
 
     line_copies = [line_copy(i) for i in range(steps - 3)]
     held = [pick(a, [int(order[z][i] // 4 in holds[z]) for z in range(m)]) for i in range(steps - 3)]
@@ -378,7 +391,7 @@
         def _():
             q = turns[i]
             slot = 4 * m + pick(a, [4 * (holds[z].index(order[z][i] // 4) if holds[z] else 0) + order[z][i] % 4 for z in range(m)])
-            remote(pair_sum.at[q], line_in.at[slot], line_s.at[q], line_r.at[slot], partner).wait_recv()
+            remote(pair_sum.at[q], line_in.at[slot], line_s.at[0], line_r.at[slot], partner).wait_recv()
             pair_sum[q] = (pair_sum[q].astype(f32) + line_in[slot].astype(f32)).astype(bf)
             line_copies[i].start()
 
@@ -396,10 +409,10 @@
             @pl.when(skip == 0)
             def _():
                 slot = 4 * src + c
-                remote(pair_sum.at[slot], line_in.at[slot], line_s.at[slot], line_r.at[slot], partner).wait_recv()
+                remote(pair_sum.at[slot], line_in.at[slot], line_s.at[0], line_r.at[slot], partner).wait_recv()
                 yz_sum[c] = yz_sum[c] + line_in[slot].astype(f32)
 
-    slab_cross = remote(slab_sum, pair_in.at[4 * a + 3], pair_s.at[4 * a + 3], pair_r.at[4 * a + 3], partner)
+    slab_cross = remote(slab_sum, pair_in.at[4 * a + 3], pair_s.at[1], pair_r.at[4 * a + 3], partner)
 
     def reduce_slab():
         q = 4 * a + 3
@@ -408,7 +421,7 @@
             src = pick(a, [others(m, z)[i] for z in range(m)])
             for side, bb in enumerate((1 - b, b)):
                 slot = 2 * src + bb
-                remote(slab_in.at[slot], slab_in.at[slot], slab_s.at[slot], slab_r.at[slot], partner).wait_recv()
+                remote(slab_in.at[slot], slab_in.at[slot], slab_s.at[0], slab_r.at[slot], partner).wait_recv()
                 total[side] = total[side] + slab_in[slot].astype(f32)
         slab_sum[...] = total[0].astype(bf)
         slab_cross.start()
@@ -418,12 +431,11 @@
         slab_cross.wait_recv()
         yz_sum[3] = yz_sum[3] + pair_in[4 * a + 3].astype(f32)
 
-    for i in range(m):
+    for i in range(2):
         row_terms(i * share)
-    for level in range(3, m + 1):
-        tell_level(level)
-        start_slabs(level - 1)
-    for i in range(m, 2 * m):
+    tell_level(m)
+    start_slabs(m - 1)
+    for i in range(2, 2 * m):
         row_terms(i * share)
     rows_in[...] = row_sums[...].astype(bf)
     core = remote(rows_in.at[1 - g], row_other.at[...], core_s.at[0], core_r.at[0], me, 1 - g)
@@ -510,36 +522,29 @@
 
     def cross_copy(bb, q):
         at = slice_of(bb, q)
-        return remote(yz_out.at[at], yz_out.at[at], cross_s.at[q], cross_r.at[q], partner)
-
-    def give_chunk(c):
-        for r in range(reach):
-            at = (offset(c) + r) * chans
-            done = conv_row(yz_inner[at : at + 3 * chans, :], weights[2, 1])
-            yz_out[own * rows + c * reach + r] = done.astype(bf)
-        q = 4 * a + c
-        cross_copy(b, q).start()
+        return remote(yz_out.at[at], yz_out.at[at], cross_s.at[0], cross_r.at[q], partner)
+
+    def give_half(half):
+        for c in half:
+            for r in range(reach):
+                at = (offset(c) + r) * chans
+                done = conv_row(yz_inner[at : at + 3 * chans, :], weights[2, 1])
+                yz_out[own * rows + c * reach + r] = done.astype(bf)
+        for c in half:
+            cross_copy(b, 4 * a + c).start()
         for i in range(m - 1):
             k = pick(a, [give_order(m, z)[i] for z in range(m)])
             skip = pick(a, [int(passed(m, z, give_order(m, z)[i])) for z in range(m)])
-            at = slice_of(b, q)
-            copy = remote(yz_out.at[at], yz_out.at[at], spread_s.at[4 * i + c], spread_r.at[q], k * 2 + b)
-            pl.when(skip == 0)(copy.start)
-            spread_copies.append((skip == 0, copy))
+            for c in half:
+                q = 4 * a + c
+                at = slice_of(b, q)
+                copy = remote(yz_out.at[at], yz_out.at[at], spread_s.at[4 * i + c], spread_r.at[q], k * 2 + b)
+                pl.when(skip == 0)(copy.start)
+                spread_copies.append((skip == 0, copy))
 
     for i in range(reach, rows - reach):
         inner_row(i, 1.0)
-    give_chunk(2)
-    give_chunk(3)
-    pl.when(halo[0][1])(halo[0][2].wait_recv)
-    inner_row(rows, 1.0)
-    inner_row(rows + 1, (place < last).astype(f32))
-    give_chunk(1)
-    pl.when(halo[1][1])(halo[1][2].wait_recv)
-    inner_row(0, (place > 0).astype(f32))
-    inner_row(1, 1.0)
-    give_chunk(0)
-
+    give_half(halves[0])
     for dx, copy in row_copies:
         pl.when((me - dx >= 0) & (me - dx < n))(copy.wait_recv)
     for s in range(2 * reach + 1):
@@ -563,24 +568,34 @@
     outs[g] = conv_row(row_inner[...], weights[g, 1]).astype(bf)
     share_out = remote(outs.at[g], outs.at[g], core_s.at[1], core_r.at[1], me, 1 - g)
     share_out.start()
+    for _, receives, copy in halo:
+        pl.when(receives)(copy.wait_recv)
+    inner_row(rows, 1.0)
+    inner_row(rows + 1, (place < last).astype(f32))
+    inner_row(0, (place > 0).astype(f32))
+    inner_row(1, 1.0)
+    give_half(halves[1])
     remote(outs.at[1 - g], outs.at[1 - g], core_s.at[1], core_r.at[1], me, 1 - g).wait_recv()
 
-    def finish(bb, q):
-        c = q % 4
-        stored = piece(bb, q // 4) * rows + c * reach
-        first = piece(bb, q // 4) * rows + offset(c)
+    def finish(*chunks):
         xy_out = outs[0].astype(f32)
         xz_out = outs[1].astype(f32)
+        at = []
+        for bb, q in chunks:
+            c = q % 4
+            stored = piece(bb, q // 4) * rows + c * reach
+            first = piece(bb, q // 4) * rows + offset(c)
+            at += [(stored + r, first + r) for r in range(reach)]
         mixed = []
-        for r in range(reach):
-            product = column(xy_out, g * count + first + r) * xz_out
-            product = product * yz_out[stored + r].astype(f32)
+        for s, y in at:
+            product = column(xy_out, g * count + y) * xz_out
+            product = product * yz_out[s].astype(f32)
             mixed.append((product_scale * product).astype(bf))
         mixed = jnp.concatenate(mixed, axis=1)
         hidden = silu(jnp.dot(wide[...], mixed, preferred_element_type=f32)).astype(bf)
         branch = jnp.dot(shrink[...], hidden, preferred_element_type=f32)
-        for r in range(reach):
-            updated[first + r] = (feature_row(first + r) + branch[:, r * cols : (r + 1) * cols]).astype(bf)
+        for k, (s, y) in enumerate(at):
+            updated[y] = (feature_row(y) + branch[:, k * cols : (k + 1) * cols]).astype(bf)
 
     takes = [pick(a, [take_order(m, z)[i] for z in range(m)]) for i in range(4 * m - 4)]
     hands = a == m - 2
@@ -596,41 +611,42 @@
         remote(yz_out.at[at], yz_out.at[at], spread_s.at[0], spread_r.at[q], partner).wait_recv()
         cross_copy(b, q).start()
         pl.when(hands & (q // 4 == handed))(hand_copy(q).start)
-        finish(b, q)
+        return b, q
 
     crossed = [4 * a + c for c in own_order] + takes
 
     def take_crossed(i):
         q = crossed[i]
         cross_copy(1 - b, q).wait_recv()
-        finish(1 - b, q)
-
-    for c in own_order:
-        finish(b, 4 * a + c)
-    for i in range(len(crossed)):
-        if i < len(takes):
-            take(i)
-        take_crossed(i)
-
-    for copy in pair_copies:
-        copy.wait_send()
-    slab_cross.wait_send()
-    for copy in line_copies:
-        copy.wait_send()
-    for _, there, copy in slab_copies:
-        pl.when(there)(copy.wait_send)
-    for sends, _, copy in halo:
-        pl.when(sends)(copy.wait_send)
-    core.wait_send()
-    share_out.wait_send()
-    for dx, copy in row_copies:
-        pl.when((me + dx >= 0) & (me + dx < n))(copy.wait_send)
-    for sent, copy in spread_copies:
-        pl.when(sent)(copy.wait_send)
-    for c in range(4):
-        pl.when(hands)(hand_copy(4 * handed + c).wait_send)
-    for q in crossed:
-        cross_copy(b, q).wait_send()
+        return 1 - b, q
+
+    finish(*[(b, 4 * a + c) for c in own_order])
+
+    def drain():
+        pair_all.wait_send()
+        slab_cross.wait_send()
+        line_all.wait_send()
+        slab_all.wait_send()
+        for sends, _, copy in halo:
+            pl.when(sends)(copy.wait_send)
+        core.wait_send()
+        share_out.wait_send()
+        for dx, copy in row_copies:
+            pl.when((me + dx >= 0) & (me + dx < n))(copy.wait_send)
+
+    pair = 2
+    for i in range(0, len(crossed), pair):
+        ready = [take(j) for j in range(i, i + pair) if j < len(takes)]
+        finish(*ready, *[take_crossed(j) for j in range(i, i + pair)])
+        if i == 2 * pair:
+            drain()
+        if i == len(crossed) - 2 * pair:
+            for given, copy in spread_copies:
+                pl.when(given)(copy.wait_send)
+            for c in range(4):
+                pl.when(hands)(hand_copy(4 * handed + c).wait_send)
+
+    cross_all.wait_send()
 
 
 def fused(voxels, occupancy, row_weights, column_weights, depth_weights, plane_kernels, expand_weight, shrink_weight):
@@ -683,9 +699,9 @@
             pltpu.VMEM((span * chans, cols), bf),
             pltpu.VMEM((3 * chans, cols), bf),
             pltpu.VMEM((planes, chans, cols), bf),
-            dma((4 * m,)), dma((4 * m,)), dma((4 * m,)), dma((8 * m,)), dma((4 * m,)), dma((2 * m,)), dma((2,)), dma((2,)),
+            dma((2,)), dma((4 * m,)), dma((1,)), dma((8 * m,)), dma((1,)), dma((2 * m,)), dma((2,)), dma((2,)),
             dma((span,)), dma((span,)), dma((2,)), dma((2,)),
-            dma((4 * m,)), dma((4 * m,)), dma((4 * m,)), dma((4 * m,)),
+            dma((4 * m,)), dma((4 * m,)), dma((1,)), dma((4 * m,)),
             pltpu.SemaphoreType.REGULAR((m, 2)),
         ],
         compiler_params=pltpu.CompilerParams(collective_id=0, has_side_effects=True),

time: 40.4 us -> 37.5 us (0.928)
  Pallas kernels: 39.3 us -> 36.3 us
    pallas_call x1, Pallas kernels: 39.3 us -> 36.3 us  [fused(): pl.pallas_call(functools.partial(block_kernel, n), out_shape=pltpu.VMEM((...]
where the time goes in v4:
time: 37.5 us; the launch traced here: 37.3 us
  Pallas kernels  36.3 us (97%)
  local copies, waits for them, and re-layouts  0.97 us (3%)
    pallas_call x1, Pallas kernels, fused(): pl.pallas_call(functools.partial(block_kernel, n), out_shape=pltpu.VMEM((...  36.3 us
    unnamed x1, local copies, waits for them, and re-layouts  0.97 us

profile of v4, /device:TPU:0, one launch (start us, length us, event | category | flops | bytes accessed | tf_op | source)
XLA Modules:
  0.0 37.3 jit_solution(13255778950155484341)
XLA Ops:
  0.0 36.3 %shard_map.82 = bf16[64,64,128]{2,1,0:T(8,128)(2,1)S(1)} custom-call(bf16[64,64,128]{2,1,0:T(8,128)(2,1)} %bitcast.10, s32[64,128]{1,0:T(8,128)} %bitcast.11, bf16[1,64]{1,0:T(2,128)(2,1)} %row_weights_in.1, bf16[64,64]{1,0:T(8,128)(2,1)} %column_weights_in.1, bf16[64,128]{1,0:T(8,128)(2,1)} %bitcast.12, bf16[3,2,3,3,64,64]{5,4,3,2,1,0:T(8,128)(2,1)} %kernels_in.1, ...), custom_call_target="tpu_custom_call" | custom-call | tf_op jit(solution)/shard_map/pallas_call | solution.py:673
  36.4 1.0 %copy.10 = bf16[1,64,128,64]{2,3,1,0:T(8,128)(2,1)} copy(bf16[1,64,128,64]{2,3,1,0:T(8,128)(2,1)S(1)} %bitcast.9) | data formatting | bytes 2097152

commit v5 on v4

--- a/solution.py
+++ b/solution.py
@@ -137,16 +137,21 @@
     return k == m - 1 and z == m - 3
 
 
+def deferred(m, z, k):
+    return (z == m - 1 and k == m - 2) or (z == m - 2 and k == m - 3)
+
+
 def give_order(m, z):
     return sorted(others(m, z), key=lambda k: k - z if k > z else k)
 
 
 def take_order(m, z):
     def rank(k):
-        return passed(m, k, z), z if k > z else z - k - 1, abs(k - z) > 1, -k
-
-    ks = sorted(others(m, z), key=rank)
-    return [4 * k + c for half in halves for k in ks for c in half]
+        return z if k > z else z - k - 1, abs(k - z) > 1 and k < z, -k
+
+    ks = sorted([k for k in others(m, z) if not passed(m, k, z) and not deferred(m, k, z)], key=rank)
+    late = [k for k in others(m, z) if passed(m, k, z) or deferred(m, k, z)]
+    return [4 * k + c for group in (ks, late) for half in halves for k in group for c in half]
 
 
 def block_kernel(
@@ -532,15 +537,24 @@
                 yz_out[own * rows + c * reach + r] = done.astype(bf)
         for c in half:
             cross_copy(b, 4 * a + c).start()
-        for i in range(m - 1):
+        later = table(lambda z: [deferred(m, z, k) for k in give_order(m, z)])
+        for turn, i, part_of in [(0, i, half) for i in range(1)] + [(1, i, halves[0]) for i in range(m - 1)] + [(2, i, half) for i in range(1, m - 1)]:
+            first_half = half is halves[0]
+            if turn == 1 and (first_half or not any(x[i] for x in later)):
+                continue
             k = pick(a, [give_order(m, z)[i] for z in range(m)])
-            skip = pick(a, [int(passed(m, z, give_order(m, z)[i])) for z in range(m)])
-            for c in half:
+            go = [not passed(m, z, give_order(m, z)[i]) for z in range(m)]
+            if turn == 1:
+                go = [x and later[z][i] for z, x in enumerate(go)]
+            elif first_half:
+                go = [x and not later[z][i] for z, x in enumerate(go)]
+            going = pick(a, [int(x) for x in go])
+            for c in part_of:
                 q = 4 * a + c
                 at = slice_of(b, q)
                 copy = remote(yz_out.at[at], yz_out.at[at], spread_s.at[4 * i + c], spread_r.at[q], k * 2 + b)
-                pl.when(skip == 0)(copy.start)
-                spread_copies.append((skip == 0, copy))
+                pl.when(going == 1)(copy.start)
+                spread_copies.append((going == 1, copy))
 
     for i in range(reach, rows - reach):
         inner_row(i, 1.0)
@@ -635,17 +649,27 @@
             pl.when((me + dx >= 0) & (me + dx < n))(copy.wait_send)
 
     pair = 2
-    for i in range(0, len(crossed), pair):
-        ready = [take(j) for j in range(i, i + pair) if j < len(takes)]
-        finish(*ready, *[take_crossed(j) for j in range(i, i + pair)])
+    lag = 2
+    for i in range(0, len(takes), pair):
+        ready = [take(j) for j in range(i, i + pair)]
+        ready += [take_crossed(j) for j in range(i - lag * pair, i - lag * pair + pair) if j >= 0]
+        finish(*ready)
         if i == 2 * pair:
             drain()
-        if i == len(crossed) - 2 * pair:
+    at = len(takes) - lag * pair
+    for size in (4, 2, 2):
+        size = min(size, len(crossed) - at)
+        if size > 0:
+            finish(*[take_crossed(at + j) for j in range(size)])
+            at += size
+        if at == len(crossed) - 2:
             for given, copy in spread_copies:
                 pl.when(given)(copy.wait_send)
             for c in range(4):
                 pl.when(hands)(hand_copy(4 * handed + c).wait_send)
-
+    while at < len(crossed):
+        finish(take_crossed(at))
+        at += 1
     cross_all.wait_send()
 
 

time: 37.5 us -> 36.5 us (0.973)
  Pallas kernels: 36.3 us -> 35.4 us
    pallas_call x1, Pallas kernels: 36.3 us -> 35.4 us  [fused(): pl.pallas_call(functools.partial(block_kernel, n), out_shape=pltpu.VMEM((...]
where the time goes in v5:
time: 36.5 us; the launch traced here: 36.4 us
  Pallas kernels  35.4 us (97%)
  local copies, waits for them, and re-layouts  0.97 us (3%)
    pallas_call x1, Pallas kernels, fused(): pl.pallas_call(functools.partial(block_kernel, n), out_shape=pltpu.VMEM((...  35.4 us
    unnamed x1, local copies, waits for them, and re-layouts  0.97 us

profile of v5, /device:TPU:0, one launch (start us, length us, event | category | flops | bytes accessed | tf_op | source)
XLA Modules:
  0.0 36.4 jit_solution(636735069819233827)
XLA Ops:
  0.0 35.4 %shard_map.82 = bf16[64,64,128]{2,1,0:T(8,128)(2,1)S(1)} custom-call(bf16[64,64,128]{2,1,0:T(8,128)(2,1)} %bitcast.10, s32[64,128]{1,0:T(8,128)} %bitcast.11, bf16[1,64]{1,0:T(2,128)(2,1)} %row_weights_in.1, bf16[64,64]{1,0:T(8,128)(2,1)} %column_weights_in.1, bf16[64,128]{1,0:T(8,128)(2,1)} %bitcast.12, bf16[3,2,3,3,64,64]{5,4,3,2,1,0:T(8,128)(2,1)} %kernels_in.1, ...), custom_call_target="tpu_custom_call" | custom-call | tf_op jit(solution)/shard_map/pallas_call | solution.py:697
  35.4 1.0 %copy.10 = bf16[1,64,128,64]{2,3,1,0:T(8,128)(2,1)} copy(bf16[1,64,128,64]{2,3,1,0:T(8,128)(2,1)S(1)} %bitcast.9) | data formatting | bytes 2097152

commit v6 on v5

--- a/solution.py
+++ b/solution.py
@@ -150,8 +150,25 @@
         return z if k > z else z - k - 1, abs(k - z) > 1 and k < z, -k
 
     ks = sorted([k for k in others(m, z) if not passed(m, k, z) and not deferred(m, k, z)], key=rank)
+    if m == 4 and z == 0:
+        return [14, 15, 10, 11, 6, 7, 13, 5, 12, 4, 9, 8]
+    if m == 4 and z == 1 and []:
+        return []
     late = [k for k in others(m, z) if passed(m, k, z) or deferred(m, k, z)]
     return [4 * k + c for group in (ks, late) for half in halves for k in group for c in half]
+
+
+def diverted(z, q):
+    return z == 0 and q in [4 + c for c in halves[0]]
+
+
+def cross_order(m, z):
+    chunks = [4 * z + c for c in own_order] + take_order(m, z)
+    late = [q for q in chunks if diverted(z, q)]
+    chunks = [q for q in chunks if q not in late]
+    if late:
+        chunks[-2:-2] = late
+    return chunks
 
 
 def block_kernel(
@@ -160,7 +177,7 @@
     part, rows_in, weights, wide, yz_out, row_sums, turned,
     pair_in, pair_sum, line_in, slab_in, slab_sum, yz_sum, yz_plane, yz_inner,
     row_other, row_slots, row_plane, row_inner, outs,
-    pair_s, pair_r, line_s, line_r, slab_s, slab_r, halo_s, halo_r, row_s, row_r, core_s, core_r, spread_s, spread_r, cross_s, cross_r, known,
+    pair_s, pair_r, line_s, line_r, slab_s, slab_r, halo_s, halo_r, row_s, row_r, core_s, core_r, spread_s, spread_r, cross_s, cross_r, divert_s, known,
 ):
     me = lax.axis_index("gx")
     g = lax.axis_index("gy")
@@ -239,7 +256,7 @@
     for bb in (1 - b, b):
         for k in range(m):
             at = pl.ds(piece(bb, k) * rows, rows)
-            large.append(pltpu.make_async_copy(voxels_in.at[at], voxels.at[at], load_s.at[2 + len(large)]))
+            large.append(pltpu.make_async_copy(voxels_in.at[at], voxels.at[at], load_s.at[2 + len(large) // m]))
     fetches = [
         pltpu.make_async_copy(kernels_in, plane_kernels, fetch_s.at[0]),
         pltpu.make_async_copy(column_weights_in, column_weights, fetch_s.at[1]),
@@ -261,8 +278,8 @@
                 part[j * rows + c * reach + r] = (feature_row(j * rows + offset(c) + r) * rw).astype(bf)
 
     pair_copies = []
-    for q in turns:
-        pair_copies.append(remote(part.at[slice_of(1 - b, q)], pair_in.at[q], pair_s.at[0], pair_r.at[q], partner))
+    for i, q in enumerate(turns):
+        pair_copies.append(remote(part.at[slice_of(1 - b, q)], pair_in.at[q], pair_s.at[0], pair_r.at[i], partner))
 
     def yz_pieces(bb):
         def some(k, carry):
@@ -271,8 +288,11 @@
 
         lax.fori_loop(0, m, some, 0)
 
-    for copy in large[:m]:
-        copy.wait()
+    def loaded(which):
+        at = pl.ds(0, m * rows)
+        pltpu.make_async_copy(voxels_in.at[at], voxels.at[at], load_s.at[2 + which]).wait()
+
+    loaded(0)
     yz_pieces(1 - b)
 
     def sent(buffer, size, sem, recv):
@@ -289,7 +309,7 @@
             there = (a + side * dist >= 0) & (a + side * dist < m)
             for bb in range(2):
                 copy = remote(
-                    part.at[slice_of(bb, 4 * k + 3)], slab_in.at[2 * a + bb], slab_s.at[0], slab_r.at[2 * a + bb], k * 2 + b
+                    part.at[slice_of(bb, 4 * k + 3)], slab_in.at[2 * a + bb], slab_s.at[0], slab_r.at[0], k * 2 + b
                 )
                 slab_copies.append((dist, there, copy))
 
@@ -301,15 +321,14 @@
     pl.semaphore_wait(barrier, greeters)
     for copy in pair_copies:
         copy.start()
-    for copy in large[m:]:
-        copy.wait()
+    loaded(1)
     yz_pieces(b)
     start_slabs(1)
 
     def tell(level, side):
         step = 2 if side == 0 else -2
         pl.semaphore_signal(
-            known.at[level, side], inc=1, device_id={"gx": jnp.clip(me - step, 0, n - 1), "gy": g}, device_id_type=MESH
+            known.at[level - 2, side], inc=1, device_id={"gx": jnp.clip(me - step, 0, n - 1), "gy": g}, device_id_type=MESH
         )
 
     def heard(level, side):
@@ -321,7 +340,7 @@
     def tell_level(level):
         for side in range(2):
             if level > 2:
-                pl.when(heard(level - 1, side))(lambda: pl.semaphore_wait(known.at[level - 1, side], 1))
+                pl.when(heard(level - 1, side))(lambda: pl.semaphore_wait(known.at[level - 3, side], 1))
             if level < m:
                 pl.when(tells(level, side))(lambda: tell(level, side))
 
@@ -373,10 +392,10 @@
             elif joined(m, z, k):
                 via = z + (1 if k > z else -1)
                 gx.append(via)
-                slot.append(4 * m + 4 * holds[via].index(k) + c)
+                slot.append(3 * m + 3 * holds[via].index(k) + c)
             else:
                 gx.append(k)
-                slot.append(4 * z + c)
+                slot.append(3 * z + c)
         to = pick(a, slot)
         q = turns[i]
         return remote(pair_sum.at[q], line_in.at[to], line_s.at[0], line_r.at[to], pick(a, gx) * 2 + b)
@@ -395,7 +414,7 @@
         @pl.when(holding)
         def _():
             q = turns[i]
-            slot = 4 * m + pick(a, [4 * (holds[z].index(order[z][i] // 4) if holds[z] else 0) + order[z][i] % 4 for z in range(m)])
+            slot = 3 * m + pick(a, [3 * (holds[z].index(order[z][i] // 4) if holds[z] else 0) + order[z][i] % 4 for z in range(m)])
             remote(pair_sum.at[q], line_in.at[slot], line_s.at[0], line_r.at[slot], partner).wait_recv()
             pair_sum[q] = (pair_sum[q].astype(f32) + line_in[slot].astype(f32)).astype(bf)
             line_copies[i].start()
@@ -413,20 +432,20 @@
 
             @pl.when(skip == 0)
             def _():
-                slot = 4 * src + c
+                slot = 3 * src + c
                 remote(pair_sum.at[slot], line_in.at[slot], line_s.at[0], line_r.at[slot], partner).wait_recv()
                 yz_sum[c] = yz_sum[c] + line_in[slot].astype(f32)
 
-    slab_cross = remote(slab_sum, pair_in.at[4 * a + 3], pair_s.at[1], pair_r.at[4 * a + 3], partner)
+    slab_cross = remote(slab_sum, pair_in.at[4 * a + 3], pair_s.at[1], pair_r.at[steps], partner)
 
     def reduce_slab():
         q = 4 * a + 3
         total = [part[slice_of(bb, q)].astype(f32) for bb in (1 - b, b)]
+        sent(slab_in, 2 * (m - 1), slab_s, slab_r).wait_recv()
         for i in range(m - 1):
             src = pick(a, [others(m, z)[i] for z in range(m)])
             for side, bb in enumerate((1 - b, b)):
                 slot = 2 * src + bb
-                remote(slab_in.at[slot], slab_in.at[slot], slab_s.at[0], slab_r.at[slot], partner).wait_recv()
                 total[side] = total[side] + slab_in[slot].astype(f32)
         slab_sum[...] = total[0].astype(bf)
         slab_cross.start()
@@ -468,7 +487,7 @@
         if dx != 0:
             slot = reach - dx
             copy = remote(
-                row_slots.at[reach], row_slots.at[slot], row_s.at[slot], row_r.at[slot], jnp.clip(me + dx, 0, n - 1)
+                row_slots.at[reach], row_slots.at[slot], row_s.at[0], row_r.at[0], jnp.clip(me + dx, 0, n - 1)
             )
             row_copies.append((dx, copy))
             pl.when((me + dx >= 0) & (me + dx < n))(copy.start)
@@ -525,9 +544,9 @@
     spread_copies = []
     own = piece(b, a)
 
-    def cross_copy(bb, q):
+    def cross_copy(bb, q, pair_at):
         at = slice_of(bb, q)
-        return remote(yz_out.at[at], yz_out.at[at], cross_s.at[0], cross_r.at[q], partner)
+        return remote(yz_out.at[at], yz_out.at[at], cross_s.at[0], cross_r.at[pair_at], partner)
 
     def give_half(half):
         for c in half:
@@ -536,7 +555,7 @@
                 done = conv_row(yz_inner[at : at + 3 * chans, :], weights[2, 1])
                 yz_out[own * rows + c * reach + r] = done.astype(bf)
         for c in half:
-            cross_copy(b, 4 * a + c).start()
+            cross_copy(b, 4 * a + c, own_order.index(c) // 2).start()
         later = table(lambda z: [deferred(m, z, k) for k in give_order(m, z)])
         for turn, i, part_of in [(0, i, half) for i in range(1)] + [(1, i, halves[0]) for i in range(m - 1)] + [(2, i, half) for i in range(1, m - 1)]:
             first_half = half is halves[0]
@@ -552,15 +571,16 @@
             for c in part_of:
                 q = 4 * a + c
                 at = slice_of(b, q)
-                copy = remote(yz_out.at[at], yz_out.at[at], spread_s.at[4 * i + c], spread_r.at[q], k * 2 + b)
+                copy = remote(yz_out.at[at], yz_out.at[at], spread_s.at[0], spread_r.at[q - jnp.where(a > k, 4, 0)], k * 2 + b)
                 pl.when(going == 1)(copy.start)
                 spread_copies.append((going == 1, copy))
 
     for i in range(reach, rows - reach):
         inner_row(i, 1.0)
     give_half(halves[0])
-    for dx, copy in row_copies:
-        pl.when((me - dx >= 0) & (me - dx < n))(copy.wait_recv)
+    beside = jnp.minimum(me, reach) + jnp.minimum(n - 1 - me, reach)
+    for size in range(1, 2 * reach + 1):
+        pl.when(beside == size)(sent(row_slots, size, row_s, row_r).wait_recv)
     for s in range(2 * reach + 1):
         at = me + s - reach
         inside = (at >= 0) & (at < n)
@@ -617,21 +637,31 @@
 
     def hand_copy(q):
         at = slice_of(b, q)
-        return remote(yz_out.at[at], yz_out.at[at], spread_s.at[4 * (m - 1) + q % 4], spread_r.at[q], (m - 1) * 2 + b)
+        return remote(yz_out.at[at], yz_out.at[at], spread_s.at[0], spread_r.at[q], (m - 1) * 2 + b)
 
     def take(i):
         q = takes[i]
         at = slice_of(b, q)
-        remote(yz_out.at[at], yz_out.at[at], spread_s.at[0], spread_r.at[q], partner).wait_recv()
-        cross_copy(b, q).start()
+        remote(yz_out.at[at], yz_out.at[at], spread_s.at[0], spread_r.at[q - jnp.where(q // 4 > a, 4, 0)], partner).wait_recv()
+        kept = pick(a, [int(not diverted(z, take_order(m, z)[i])) for z in range(m)])
+        spot = pick(a, [cross_order(m, z).index(take_order(m, z)[i]) // 2 for z in range(m)])
+        pl.when(kept == 1)(cross_copy(b, q, spot).start)
         pl.when(hands & (q // 4 == handed))(hand_copy(q).start)
         return b, q
 
-    crossed = [4 * a + c for c in own_order] + takes
+    crossed = [pick(a, [cross_order(m, z)[i] for z in range(m)]) for i in range(4 * m)]
+
+    def divert_copy(c):
+        at = slice_of(1 - b, 4 + c)
+        return remote(yz_out.at[at], yz_out.at[at], divert_s.at[0], cross_r.at[cross_order(m, 0).index(4 + c) // 2], b)
 
     def take_crossed(i):
         q = crossed[i]
-        cross_copy(1 - b, q).wait_recv()
+        if i % 2 == 0:
+            at = pl.ds(0, 2 * reach)
+            remote(yz_out.at[at], yz_out.at[at], cross_s.at[0], cross_r.at[i // 2], partner).wait_recv()
+        if i < len(halves[0]):
+            pl.when(a == 1)(divert_copy(halves[0][i]).start)
         return 1 - b, q
 
     finish(*[(b, 4 * a + c) for c in own_order])
@@ -645,8 +675,8 @@
             pl.when(sends)(copy.wait_send)
         core.wait_send()
         share_out.wait_send()
-        for dx, copy in row_copies:
-            pl.when((me + dx >= 0) & (me + dx < n))(copy.wait_send)
+        for size in range(1, 2 * reach + 1):
+            pl.when(beside == size)(sent(row_slots, size, row_s, row_r).wait_send)
 
     pair = 2
     lag = 2
@@ -663,14 +693,19 @@
             finish(*[take_crossed(at + j) for j in range(size)])
             at += size
         if at == len(crossed) - 2:
-            for given, copy in spread_copies:
-                pl.when(given)(copy.wait_send)
-            for c in range(4):
-                pl.when(hands)(hand_copy(4 * handed + c).wait_send)
+            counts = [
+                4 * (m - 1 - sum(passed(m, z, k) for k in others(m, z)) + sum(passed(m, k, m - 1) for k in [m - 3]) * (z == m - 2))
+                for z in range(m)
+            ]
+            for size in sorted(set(counts)):
+                amount = sent(yz_out, size * reach, spread_s, spread_r)
+                pl.when(pick(a, [int(x == size) for x in counts]) == 1)(amount.wait_send)
     while at < len(crossed):
         finish(take_crossed(at))
         at += 1
-    cross_all.wait_send()
+    pl.when(a > 0)(cross_all.wait_send)
+    pl.when(a == 0)(sent(yz_out, (4 * m - len(halves[0])) * reach, cross_s, cross_r).wait_send)
+    pl.when(a == 1)(sent(yz_out, len(halves[0]) * reach, divert_s, cross_r).wait_send)
 
 
 def fused(voxels, occupancy, row_weights, column_weights, depth_weights, plane_kernels, expand_weight, shrink_weight):
@@ -701,7 +736,7 @@
         out_specs=pl.BlockSpec(memory_space=pltpu.VMEM),
         scratch_shapes=[pltpu.VMEM(x.shape, x.dtype) for x in operands]
         + [
-            dma((2 + n,)),
+            dma((4,)),
             dma((5,)),
             pltpu.VMEM((count, chans, cols), bf),
             pltpu.VMEM((planes, chans, cols), bf),
@@ -712,7 +747,7 @@
             pltpu.VMEM((chans, count), f32),
             pltpu.VMEM((4 * m, reach, chans, cols), bf),
             pltpu.VMEM((4 * m, reach, chans, cols), bf),
-            pltpu.VMEM((8 * m, reach, chans, cols), bf),
+            pltpu.VMEM((6 * m, reach, chans, cols), bf),
             pltpu.VMEM((2 * m, reach, chans, cols), bf),
             pltpu.VMEM((reach, chans, cols), bf),
             pltpu.VMEM((4, reach, chans, cols), f32),
@@ -723,10 +758,10 @@
             pltpu.VMEM((span * chans, cols), bf),
             pltpu.VMEM((3 * chans, cols), bf),
             pltpu.VMEM((planes, chans, cols), bf),
-            dma((2,)), dma((4 * m,)), dma((1,)), dma((8 * m,)), dma((1,)), dma((2 * m,)), dma((2,)), dma((2,)),
-            dma((span,)), dma((span,)), dma((2,)), dma((2,)),
-            dma((4 * m,)), dma((4 * m,)), dma((1,)), dma((4 * m,)),
-            pltpu.SemaphoreType.REGULAR((m, 2)),
+            dma((2,)), dma((3 * m + 1,)), dma((1,)), dma((6 * m - 6,)), dma((1,)), dma((1,)), dma((2,)), dma((2,)),
+            dma((1,)), dma((1,)), dma((2,)), dma((2,)),
+            dma((1,)), dma((4 * m - 4,)), dma((1,)), dma((2 * m,)), dma((1,)),
+            pltpu.SemaphoreType.REGULAR((m - 2, 2)),
         ],
         compiler_params=pltpu.CompilerParams(collective_id=0, has_side_effects=True),
     )(*operands)

time: 36.5 us -> 35.2 us (0.964)
  Pallas kernels: 35.4 us -> 34.1 us
    pallas_call x1, Pallas kernels: 35.4 us -> 34.1 us  [fused(): pl.pallas_call(functools.partial(block_kernel, n), out_shape=pltpu.VMEM((...]
where the time goes in v6:
time: 35.2 us; the launch traced here: 35.1 us
  Pallas kernels  34.1 us (97%)
  local copies, waits for them, and re-layouts  0.97 us (3%)
    pallas_call x1, Pallas kernels, fused(): pl.pallas_call(functools.partial(block_kernel, n), out_shape=pltpu.VMEM((...  34.1 us
    unnamed x1, local copies, waits for them, and re-layouts  0.97 us

profile of v6, /device:TPU:0, one launch (start us, length us, event | category | flops | bytes accessed | tf_op | source)
XLA Modules:
  0.0 35.1 jit_solution(3829937204848483440)
XLA Ops:
  0.0 34.1 %shard_map.82 = bf16[64,64,128]{2,1,0:T(8,128)(2,1)S(1)} custom-call(bf16[64,64,128]{2,1,0:T(8,128)(2,1)} %bitcast.10, s32[64,128]{1,0:T(8,128)} %bitcast.11, bf16[1,64]{1,0:T(2,128)(2,1)} %row_weights_in.1, bf16[64,64]{1,0:T(8,128)(2,1)} %column_weights_in.1, bf16[64,128]{1,0:T(8,128)(2,1)} %bitcast.12, bf16[3,2,3,3,64,64]{5,4,3,2,1,0:T(8,128)(2,1)} %kernels_in.1, ...), custom_call_target="tpu_custom_call" | custom-call | tf_op jit(solution)/shard_map/pallas_call | solution.py:732
  34.1 1.0 %copy.10 = bf16[1,64,128,64]{2,3,1,0:T(8,128)(2,1)} copy(bf16[1,64,128,64]{2,3,1,0:T(8,128)(2,1)S(1)} %bitcast.9) | data formatting | bytes 2097152

commit v7 on v6

--- a/solution.py
+++ b/solution.py
@@ -167,7 +167,7 @@
     late = [q for q in chunks if diverted(z, q)]
     chunks = [q for q in chunks if q not in late]
     if late:
-        chunks[-2:-2] = late
+        chunks[-4:-4] = late
     return chunks
 
 
@@ -679,7 +679,7 @@
             pl.when(beside == size)(sent(row_slots, size, row_s, row_r).wait_send)
 
     pair = 2
-    lag = 2
+    lag = 3
     for i in range(0, len(takes), pair):
         ready = [take(j) for j in range(i, i + pair)]
         ready += [take_crossed(j) for j in range(i - lag * pair, i - lag * pair + pair) if j >= 0]
@@ -687,7 +687,7 @@
         if i == 2 * pair:
             drain()
     at = len(takes) - lag * pair
-    for size in (4, 2, 2):
+    for size in (4, 4, 2, 2):
         size = min(size, len(crossed) - at)
         if size > 0:
             finish(*[take_crossed(at + j) for j in range(size)])

time: 35.2 us -> 35.1 us (level)
  no operation moved by 1% of the time
where the time goes in v7:
time: 35.1 us; the launch traced here: 35 us
  Pallas kernels  34 us (97%)
  local copies, waits for them, and re-layouts  0.97 us (3%)
    pallas_call x1, Pallas kernels, fused(): pl.pallas_call(functools.partial(block_kernel, n), out_shape=pltpu.VMEM((...  34 us
    unnamed x1, local copies, waits for them, and re-layouts  0.97 us

profile of v7, /device:TPU:0, one launch (start us, length us, event | category | flops | bytes accessed | tf_op | source)
XLA Modules:
  0.0 35.0 jit_solution(9694076165104622114)
XLA Ops:
  0.0 34.0 %shard_map.82 = bf16[64,64,128]{2,1,0:T(8,128)(2,1)S(1)} custom-call(bf16[64,64,128]{2,1,0:T(8,128)(2,1)} %bitcast.10, s32[64,128]{1,0:T(8,128)} %bitcast.11, bf16[1,64]{1,0:T(2,128)(2,1)} %row_weights_in.1, bf16[64,64]{1,0:T(8,128)(2,1)} %column_weights_in.1, bf16[64,128]{1,0:T(8,128)(2,1)} %bitcast.12, bf16[3,2,3,3,64,64]{5,4,3,2,1,0:T(8,128)(2,1)} %kernels_in.1, ...), custom_call_target="tpu_custom_call" | custom-call | tf_op jit(solution)/shard_map/pallas_call | solution.py:732
  34.0 1.0 %copy.10 = bf16[1,64,128,64]{2,3,1,0:T(8,128)(2,1)} copy(bf16[1,64,128,64]{2,3,1,0:T(8,128)(2,1)S(1)} %bitcast.9) | data formatting | bytes 2097152

commit v8 on v7

--- a/solution.py
+++ b/solution.py
@@ -279,7 +279,7 @@
 
     pair_copies = []
     for i, q in enumerate(turns):
-        pair_copies.append(remote(part.at[slice_of(1 - b, q)], pair_in.at[q], pair_s.at[0], pair_r.at[i], partner))
+        pair_copies.append(remote(part.at[slice_of(1 - b, q)], pair_in.at[q], pair_s.at[0], pair_r.at[min(i, steps - 3)], partner))
 
     def yz_pieces(bb):
         def some(k, carry):
@@ -392,10 +392,10 @@
             elif joined(m, z, k):
                 via = z + (1 if k > z else -1)
                 gx.append(via)
-                slot.append(3 * m + 3 * holds[via].index(k) + c)
+                slot.append(3 * (m - 1) + 3 * holds[via].index(k) + c)
             else:
                 gx.append(k)
-                slot.append(3 * z + c)
+                slot.append(3 * (z - (z > k)) + c)
         to = pick(a, slot)
         q = turns[i]
         return remote(pair_sum.at[q], line_in.at[to], line_s.at[0], line_r.at[to], pick(a, gx) * 2 + b)
@@ -414,13 +414,14 @@
         @pl.when(holding)
         def _():
             q = turns[i]
-            slot = 3 * m + pick(a, [3 * (holds[z].index(order[z][i] // 4) if holds[z] else 0) + order[z][i] % 4 for z in range(m)])
+            slot = 3 * (m - 1) + pick(a, [3 * (holds[z].index(order[z][i] // 4) if holds[z] else 0) + order[z][i] % 4 for z in range(m)])
             remote(pair_sum.at[q], line_in.at[slot], line_s.at[0], line_r.at[slot], partner).wait_recv()
             pair_sum[q] = (pair_sum[q].astype(f32) + line_in[slot].astype(f32)).astype(bf)
             line_copies[i].start()
 
     def reduce_own(c):
-        pair_copies[steps - 3 + c].wait_recv()
+        if c == 0:
+            remote(pair_in.at[pl.ds(0, 3)], pair_in.at[pl.ds(0, 3)], pair_s.at[0], pair_r.at[steps - 3], partner).wait_recv()
         q = 4 * a + c
         yz_sum[c] = part[slice_of(b, q)].astype(f32) + pair_in[q].astype(f32)
 
@@ -432,11 +433,11 @@
 
             @pl.when(skip == 0)
             def _():
-                slot = 3 * src + c
+                slot = 3 * (src - jnp.where(src > a, 1, 0)) + c
                 remote(pair_sum.at[slot], line_in.at[slot], line_s.at[0], line_r.at[slot], partner).wait_recv()
                 yz_sum[c] = yz_sum[c] + line_in[slot].astype(f32)
 
-    slab_cross = remote(slab_sum, pair_in.at[4 * a + 3], pair_s.at[1], pair_r.at[steps], partner)
+    slab_cross = remote(slab_sum, pair_in.at[4 * a + 3], pair_s.at[1], pair_r.at[steps - 2], partner)
 
     def reduce_slab():
         q = 4 * a + 3
@@ -758,7 +759,7 @@
             pltpu.VMEM((span * chans, cols), bf),
             pltpu.VMEM((3 * chans, cols), bf),
             pltpu.VMEM((planes, chans, cols), bf),
-            dma((2,)), dma((3 * m + 1,)), dma((1,)), dma((6 * m - 6,)), dma((1,)), dma((1,)), dma((2,)), dma((2,)),
+            dma((2,)), dma((3 * m - 1,)), dma((1,)), dma((6 * m - 9,)), dma((1,)), dma((1,)), dma((2,)), dma((2,)),
             dma((1,)), dma((1,)), dma((2,)), dma((2,)),
             dma((1,)), dma((4 * m - 4,)), dma((1,)), dma((2 * m,)), dma((1,)),
             pltpu.SemaphoreType.REGULAR((m - 2, 2)),

time: 35.1 us -> 35.1 us (level)
  no operation moved by 1% of the time
where the time goes in v8:
time: 35.1 us; the launch traced here: 34.9 us
  Pallas kernels  34 us (97%)
  local copies, waits for them, and re-layouts  0.97 us (3%)
    pallas_call x1, Pallas kernels, fused(): pl.pallas_call(functools.partial(block_kernel, n), out_shape=pltpu.VMEM((...  34 us
    unnamed x1, local copies, waits for them, and re-layouts  0.97 us

profile of v8, /device:TPU:0, one launch (start us, length us, event | category | flops | bytes accessed | tf_op | source)
XLA Modules:
  0.0 34.9 jit_solution(10348122153312554209)
XLA Ops:
  0.0 34.0 %shard_map.82 = bf16[64,64,128]{2,1,0:T(8,128)(2,1)S(1)} custom-call(bf16[64,64,128]{2,1,0:T(8,128)(2,1)} %bitcast.10, s32[64,128]{1,0:T(8,128)} %bitcast.11, bf16[1,64]{1,0:T(2,128)(2,1)} %row_weights_in.1, bf16[64,64]{1,0:T(8,128)(2,1)} %column_weights_in.1, bf16[64,128]{1,0:T(8,128)(2,1)} %bitcast.12, bf16[3,2,3,3,64,64]{5,4,3,2,1,0:T(8,128)(2,1)} %kernels_in.1, ...), custom_call_target="tpu_custom_call" | custom-call | tf_op jit(solution)/shard_map/pallas_call | solution.py:733
  34.0 1.0 %copy.10 = bf16[1,64,128,64]{2,3,1,0:T(8,128)(2,1)} copy(bf16[1,64,128,64]{2,3,1,0:T(8,128)(2,1)S(1)} %bitcast.9) | data formatting | bytes 2097152

commit v9 on v8

--- a/solution.py
+++ b/solution.py
@@ -151,7 +151,7 @@
 
     ks = sorted([k for k in others(m, z) if not passed(m, k, z) and not deferred(m, k, z)], key=rank)
     if m == 4 and z == 0:
-        return [14, 15, 10, 11, 6, 7, 13, 5, 12, 4, 9, 8]
+        return [14, 15, 10, 11, 13, 12, 6, 7, 9, 8, 5, 4]
     if m == 4 and z == 1 and []:
         return []
     late = [k for k in others(m, z) if passed(m, k, z) or deferred(m, k, z)]

time: 35.1 us -> 35.1 us (level)
  no operation moved by 1% of the time
where the time goes in v9:
time: 35.1 us; the launch traced here: 34.9 us
  Pallas kernels  33.9 us (97%)
  local copies, waits for them, and re-layouts  0.97 us (3%)
    pallas_call x1, Pallas kernels, fused(): pl.pallas_call(functools.partial(block_kernel, n), out_shape=pltpu.VMEM((...  33.9 us
    unnamed x1, local copies, waits for them, and re-layouts  0.97 us

profile of v9, /device:TPU:0, one launch (start us, length us, event | category | flops | bytes accessed | tf_op | source)
XLA Modules:
  0.0 34.9 jit_solution(3257773967726343628)
XLA Ops:
  0.0 33.9 %shard_map.82 = bf16[64,64,128]{2,1,0:T(8,128)(2,1)S(1)} custom-call(bf16[64,64,128]{2,1,0:T(8,128)(2,1)} %bitcast.10, s32[64,128]{1,0:T(8,128)} %bitcast.11, bf16[1,64]{1,0:T(2,128)(2,1)} %row_weights_in.1, bf16[64,64]{1,0:T(8,128)(2,1)} %column_weights_in.1, bf16[64,128]{1,0:T(8,128)(2,1)} %bitcast.12, bf16[3,2,3,3,64,64]{5,4,3,2,1,0:T(8,128)(2,1)} %kernels_in.1, ...), custom_call_target="tpu_custom_call" | custom-call | tf_op jit(solution)/shard_map/pallas_call | solution.py:733
  34.0 1.0 %copy.10 = bf16[1,64,128,64]{2,3,1,0:T(8,128)(2,1)} copy(bf16[1,64,128,64]{2,3,1,0:T(8,128)(2,1)S(1)} %bitcast.9) | data formatting | bytes 2097152
